TPU v7x, 256 devices: a whole 4x4x8 slice. The times are simulated.
256 devices in a mesh: grp: 4 (over y), dev: 64 (over x, z, core).
Axes of the slice: x: 4, y: 4, z: 8, core: 2. Of those that a mesh axis runs over, the one named last changes fastest.
Arguments:
- field: float32 [512, 512, 256, 4], P('dev', 'grp'), may hold values from -21 to 21
- start_basis: float32 [512, 64], replicated, may hold values from -6 to 6
Outputs:
- factor: float32 [512, 64], replicated
- core: float32 [64, 512, 256, 4], P(None, ('grp', 'dev'))
All inputs are finite; a program needn't handle non-finite values.
Results may differ from a plain program's by a relative error of at most 0.0003.
Values sent between devices are 32-bit elements; how exact they have to be, the bound alone decides.
No kernel may reach another device: no remote copies, remote signals or barrier semaphores. Data moves between devices by JAX's collectives and lax.ppermute only.
A program may use at most 192 MiB of HBM per device.

v0:
```python
import jax
import jax.numpy as jnp
from jax import lax
from jax.sharding import PartitionSpec as P

ITERS = 3


def product(left, right):
    return jnp.dot(left, right, precision=lax.Precision.HIGHEST, preferred_element_type=jnp.float32)


def on_device(field, start_basis):
    regrouped = lax.all_to_all(field, "dev", split_axis=1, concat_axis=0, tiled=True)
    rows = regrouped.shape[0]
    local_cols = regrouped.shape[1] * regrouped.shape[2] * regrouped.shape[3]
    unfold = regrouped.reshape(rows, local_cols)
    local_gram = product(unfold, unfold.T)
    gram = lax.psum(local_gram, ("grp", "dev"))
    basis = start_basis
    for step in range(ITERS):
        image = product(gram, basis)
        cross = product(image.T, image)
        chol = jnp.linalg.cholesky(cross)
        basis = lax.linalg.triangular_solve(
            chol, image, left_side=False, lower=True, transpose_a=True
        )
    core = product(basis.T, unfold)
    return (
        basis,
        core.reshape(basis.shape[1], regrouped.shape[1], regrouped.shape[2], regrouped.shape[3]),
    )


def solution(mesh):
    placed = (P("dev", "grp", None, None), P())
    return jax.shard_map(
        on_device,
        mesh=mesh,
        in_specs=placed,
        out_specs=(P(), P(None, ("grp", "dev"), None, None)),
        check_vma=False,
    )
```

profile of v0, /device:TPU:1, one launch (start us, length us, event | category | flops | bytes accessed | tf_op | source)
XLA Modules:
  0.0 543.2 jit_solution(3584140676412488919)
XLA Ops:
  7.2 3.4 copy.14
  10.7 109.0 %all_to_all.15 = f32[8,128,256,4]{2,3,0,1:T(4,128)} all-to-all(f32[8,128,256,4]{2,3,0,1:T(4,128)S(1)} %copy.14), channel_id=1, replica_groups=mesh['grp'=4,'dev'=64] {'dev'}, dimensions={1} | all-to-all | bytes 8388608 | tf_op jit(solution)/shard_map/all_to_all | solution.py:14
  119.7 50.4 %copy.15 = f32[8,64,2,256,4]{0,1,4,3,2:T(8,128)} copy(f32[8,64,2,256,4]{3,4,0,2,1:T(4,128)} %bitcast.63) | data formatting | bytes 8388608 | tf_op jit(solution)/shard_map/all_to_all | solution.py:14
  170.1 48.3 %reshape.21 = f32[512,2048]{0,1:T(8,128)} reshape(f32[64,8,2,256,4]{1,0,4,3,2:T(8,128)} %bitcast.1) | data formatting | bytes 8388608 | tf_op jit(solution)/shard_map/reshape | solution.py:17
  218.4 11.3 %fusion.17 = f32[512,512]{1,0:T(8,128)} fusion(f32[512,2048]{0,1:T(8,128)} %reshape.21), kind=kOutput, calls=%fused_computation.31 | convolution fusion | flops 6442450944 | bytes 5242880 | tf_op jit(solution)/shard_map/dot_general | solution.py:10
  229.8 5.2 dot_general.36
  234.9 248.8 %all-reduce.2.cloned.1.call-done = f32[512,512]{1,0:T(8,128)} async-done(((f32[512,512]{1,0:T(8,128)}), f32[512,512]{1,0:T(8,128)}) %all-reduce.2.cloned.1.call-update) | async-done | bytes 1048592 | tf_op jit(solution)/shard_map/psum | solution.py:19
  483.7 2.4 fusion.18
  486.6 5.8 %cholesky.59 = f32[64,64]{1,0:T(8,128)S(1)} custom-call(f32[64,64]{1,0:T(8,128)S(1)} %fusion.12), custom_call_target="Cholesky" | custom-call | tf_op jit(solution)/shard_map/jit(cholesky)/cholesky | solution.py:24
  492.4 0.6 compare_reduce_fusion.2
  493.1 0.7 fusion.3
  493.7 4.9 custom-call.7
  499.0 2.4 fusion.20
  501.7 5.8 %cholesky.70 = f32[64,64]{1,0:T(8,128)S(1)} custom-call(f32[64,64]{1,0:T(8,128)S(1)} %fusion.10), custom_call_target="Cholesky" | custom-call | tf_op jit(solution)/shard_map/jit(cholesky)/cholesky | solution.py:24
  507.6 0.6 compare_reduce_fusion.1
  508.2 0.7 fusion.4
  508.9 4.9 custom-call.8
  514.1 1.1 fusion.22
  515.6 5.8 %cholesky.81 = f32[64,64]{1,0:T(8,128)S(1)} custom-call(f32[64,64]{1,0:T(8,128)S(1)} %fusion.8), custom_call_target="Cholesky" | custom-call | tf_op jit(solution)/shard_map/jit(cholesky)/cholesky | solution.py:24
  521.5 0.6 compare_reduce_fusion
  522.2 0.7 fusion.5
  522.8 4.9 custom-call.9
  528.1 7.1 %fusion = f32[64,2,256,4]{2,0,3,1:T(8,128)S(1)} fusion(f32[2,256,4,512]{3,2,1,0:T(4,128)} %dot_general.36, f32[64,512]{1,0:T(8,128)S(1)} %fusion.6), kind=kOutput, calls=%fused_computation | convolution fusion | flops 805306368 | bytes 4849664 | tf_op jit(solution)/shard_map/dot_general | solution.py:10
  535.2 1.1 copy.20
  (23 shorter events, 2.2 us)
Async XLA Ops:
  7.2 476.6 %copy-start = (f32[512,64]{0,1:T(8,128)S(1)}, f32[512,64]{0,1:T(8,128)}, u32[]{:S(2)}) copy-start(f32[512,64]{0,1:T(8,128)} %param.6) | copy-start | bytes 393220
  7.2 476.6 %all-reduce.2.cloned.1.call-start = ((), (), s32[]{:S(2)}) async-start(), calls=%async_computation.1 | async-start | bytes 2097152 | tf_op jit(solution)/shard_map/psum | solution.py:19
  483.7 30.4 %copy-start.1 = (f32[512,512]{1,0:T(8,128)S(1)}, f32[512,512]{1,0:T(8,128)}, u32[]{:S(2)}) copy-start(f32[512,512]{1,0:T(8,128)} %all-reduce.2.cloned.1.call-done) | copy-start | bytes 3145732
  528.1 8.3 %copy-start.2 = (f32[64,512]{1,0:T(8,128)}, f32[64,512]{1,0:T(8,128)S(1)}, u32[]{:S(2)}) copy-start(f32[64,512]{1,0:T(8,128)S(1)} %fusion.6) | copy-start | bytes 393220
Sparse Core Ops, SparseCore 0:
  229.9 253.8 all-reduce.1
where the time goes:
time: 545 us; the launch traced here: 543 us
  waiting for transfers between devices  249 us (46%)
  local copies, waits for them, and re-layouts  109 us (20%)
  blocking collectives  109 us (20%)
  other arithmetic  36.2 us (7%)
  matrix products  26.2 us (5%)
  between operations  14.2 us (3%)
    psum x1, waiting for transfers between devices, on_device(): gram = lax.psum(local_gram, ('grp', 'dev'))  249 us
    all_to_all x1, blocking collectives, on_device(): lax.all_to_all(field, 'dev', split_axis=1, concat_axis=0, tiled=True)  109 us
    all_to_all x1, local copies, waits for them, and re-layouts, on_device(): lax.all_to_all(field, 'dev', split_axis=1, concat_axis=0, tiled=True)  50.4 us
    reshape x1, local copies, waits for them, and re-layouts, on_device(): unfold = regrouped.reshape(rows, local_cols)  48.3 us
    dot_general x8, matrix products, product(): jnp.dot(left, right, precision=lax.Precision.HIGHEST, preferred_element_t...  25.2 us
    another operation x9, other arithmetic, on_device(): chol = jnp.linalg.cholesky(cross)  19.6 us
    another operation x6, other arithmetic, on_device(): lax.linalg.triangular_solve(chol, image, left_side=False, lower=True, tra...  16.6 us
  transfers between devices with their start and end apart: 1, of which 1 were waited for; matrix products, arithmetic and copies ran while one was open for 1% of the time, Pallas kernels for 0%

commit v1 on v0

v1 whole, which is shorter than its diff:
```python
import jax
import jax.numpy as jnp
from jax import lax
from jax.experimental import pallas as pl
from jax.experimental.pallas import tpu as pltpu
from jax.experimental.layout import Layout, with_layout_constraint
from jax.sharding import Mesh, PartitionSpec as P

ITERS = 3
LANES = 128
PACK = tuple((i, j) for i in range(4) for j in range(i, 4))
VMEM = pltpu.VMEM
HIGHEST = lax.Precision.HIGHEST


def dot_nt(left, right, precision=None):
    return lax.dot_general(
        left, right, (((1,), (1,)), ((), ())),
        precision=precision, preferred_element_type=jnp.float32,
    )


def dot_nn(left, right, precision=None):
    return lax.dot_general(
        left, right, (((1,), (0,)), ((), ())),
        precision=precision, preferred_element_type=jnp.float32,
    )


def gather_columns(x_ref, rows):
    return jnp.concatenate(
        [x_ref[:, pl.ds(c, 8, stride=8), :].reshape(rows, LANES) for c in range(8)], axis=1
    )


def split(x):
    high = x.astype(jnp.bfloat16)
    mid = (x - high.astype(jnp.float32)).astype(jnp.bfloat16)
    return high, mid


def gram_kernel(x_ref, packed_ref, square, mixed):
    step = pl.program_id(0)
    x = gather_columns(x_ref, 512)
    high, mid = split(x)
    square_step = dot_nt(high, high)
    mixed_step = dot_nt(high, mid) + 0.5 * dot_nt(mid, mid)

    @pl.when(step == 0)
    def _():
        square[...] = square_step
        mixed[...] = mixed_step

    @pl.when(step == pl.num_programs(0) - 1)
    def _():
        both = mixed[...] + mixed_step
        whole = square[...] + square_step + both + both.T
        for n, (i, j) in enumerate(PACK):
            packed_ref[n] = whole[i * LANES:(i + 1) * LANES, j * LANES:(j + 1) * LANES]


def local_gram(blocks):
    return pl.pallas_call(
        gram_kernel,
        grid=(2,),
        in_specs=[pl.BlockSpec((64, None, 64, LANES), lambda i: (0, i, 0, 0))],
        out_specs=pl.BlockSpec((len(PACK), LANES, LANES), lambda i: (0, 0, 0)),
        out_shape=jax.ShapeDtypeStruct((len(PACK), LANES, LANES), jnp.float32),
        scratch_shapes=[VMEM((512, 512), jnp.float32), VMEM((512, 512), jnp.float32)],
        name="local_gram",
    )(blocks)


def inverse_cholesky(cross):
    n = cross.shape[0]
    row_id = lax.broadcasted_iota(jnp.int32, (n, n), 0)
    col_id = lax.broadcasted_iota(jnp.int32, (n, n), 1)
    work = jnp.concatenate([cross, (row_id == col_id).astype(jnp.float32)], axis=1)
    rows = lax.broadcasted_iota(jnp.int32, (n, 2 * n), 0)
    out = []
    for k in range(0, n, 2):
        first, second = work[k:k + 1, :], work[k + 1:k + 2, :]
        a, b, c = first[:, k:k + 1], first[:, k + 1:k + 2], second[:, k + 1:k + 2]
        ratio = b / a
        rest = c - b * ratio
        second = second - ratio * first
        out.append(first / jnp.sqrt(a))
        out.append(second / jnp.sqrt(rest))
        if k + 2 < n:
            base = (k + 2) // 8 * 8
            tail = work[base:, :]
            one = tail[:, k:k + 1]
            two = tail[:, k + 1:k + 2] - ratio * one
            update = tail - (one / a) * first - (two / rest) * second
            tail = jnp.where(rows[base:, :] > k + 1, update, tail)
            work = tail if base == 0 else jnp.concatenate([work[:base], tail], axis=0)
    return jnp.concatenate(out, axis=0)[:, n:]


def subspace_kernel(core_ref, mine_ref, other_ref, start_ref, out_ref, packed, gram):
    core = core_ref[0]
    packed[core] = mine_ref[...]
    packed[1 - core] = other_ref[...]
    for n, (i, j) in enumerate(PACK):
        block = packed[n // 5, n % 5]
        gram[i * LANES:(i + 1) * LANES, j * LANES:(j + 1) * LANES] = block
        if i != j:
            gram[j * LANES:(j + 1) * LANES, i * LANES:(i + 1) * LANES] = block.T
    basis = start_ref[...]
    for _ in range(ITERS):
        image = dot_nn(basis, gram[...], HIGHEST)
        image = image * lax.rsqrt(jnp.sum(image * image, axis=1, keepdims=True))
        cross = dot_nt(image, image, HIGHEST)
        basis = dot_nn(inverse_cholesky(cross), image, HIGHEST)
    out_ref[...] = basis


def subspace(core, mine, other, start):
    whole = pl.BlockSpec(memory_space=VMEM)
    return pl.pallas_call(
        subspace_kernel,
        in_specs=[pl.BlockSpec(memory_space=pltpu.SMEM), whole, whole, whole],
        out_specs=whole,
        out_shape=jax.ShapeDtypeStruct(start.shape, jnp.float32),
        scratch_shapes=[
            VMEM((2, 5, LANES, LANES), jnp.float32),
            VMEM((512, 512), jnp.float32),
        ],
        name="subspace",
    )(core, mine, other, start)


def core_kernel(basis_ref, x_ref, out_ref):
    x = gather_columns(x_ref, 512)
    core = dot_nn(basis_ref[...], x, HIGHEST)
    rank = core.shape[0]
    flat = out_ref.reshape(rank * 8, LANES)
    for c in range(8):
        flat[pl.ds(c, rank, stride=8), :] = core[:, c * LANES:(c + 1) * LANES]


def project(basis, blocks):
    rank = basis.shape[0]
    return pl.pallas_call(
        core_kernel,
        grid=(2,),
        in_specs=[
            pl.BlockSpec((rank, 512), lambda i: (0, 0)),
            pl.BlockSpec((64, None, 64, LANES), lambda i: (0, i, 0, 0)),
        ],
        out_specs=pl.BlockSpec((rank, None, 8, LANES), lambda i: (0, i, 0, 0)),
        out_shape=jax.ShapeDtypeStruct((rank, 2, 8, LANES), jnp.float32),
        name="project",
    )(basis, blocks)


def exchange(x, axes):
    return lax.all_to_all(x, axes, split_axis=0, concat_axis=0, tiled=True)


def sum_over_devices(packed):
    swap = [(0, 1), (1, 0)]
    core = lax.axis_index("c")
    flat = packed.reshape(2, 640, LANES)
    theirs = lax.ppermute(flat, "c", swap)
    half = lax.dynamic_index_in_dim(flat, core, 0, False) + lax.dynamic_index_in_dim(theirs, core, 0, False)
    parts = exchange(half.reshape(16, 40, LANES), ("y", "x"))
    part = jnp.sum(parts, axis=0)
    parts = exchange(jnp.broadcast_to(part[None], (8, 40, LANES)), "z")
    part = jnp.sum(parts, axis=0)
    half = exchange(jnp.broadcast_to(part[None], (16, 40, LANES)), ("y", "x"))
    mine = half.reshape(5, LANES, LANES)
    other = lax.ppermute(mine, "c", swap)
    return core, mine, other


def on_device(field, start_basis):
    rows, cols = field.shape[0], field.shape[1]
    view = field.reshape(rows, cols, 2, LANES, 4)
    view = with_layout_constraint(view, Layout(major_to_minor=(0, 1, 2, 4, 3)))
    view = view.transpose(1, 0, 2, 4, 3).reshape(cols, rows, 8, LANES)
    moved = exchange(view, ("x", "z", "c"))
    blocks = moved.reshape(64, cols // 64, rows * 8, LANES)
    packed = local_gram(blocks)
    core, mine, other = sum_over_devices(packed)
    basis = subspace(core.reshape(1), mine, other, start_basis.T)
    out = project(basis, blocks)
    rank = basis.shape[0]
    out = out.reshape(rank, cols // 64, 2, 4, LANES).transpose(0, 1, 2, 4, 3)
    return basis.T, out.reshape(rank, cols // 64, 256, 4)


def solution(mesh):
    fine = Mesh(mesh.devices.reshape(4, 4, 8, 2), ("y", "x", "z", "c"))
    return jax.shard_map(
        on_device,
        mesh=fine,
        in_specs=(P(("x", "z", "c"), "y", None, None), P()),
        out_specs=(P(), P(None, ("y", "x", "z", "c"), None, None)),
        check_vma=False,
    )
```

time: 545 us -> 192 us (0.35)
  waiting for transfers between devices: 249 us -> 3.19 us
  local copies, waits for them, and re-layouts: 109 us -> 3.51 us
  blocking collectives: 109 us -> 146 us
  other arithmetic: 36.2 us -> 1.05 us
  Pallas kernels: 0 us -> 33.5 us
  matrix products: 26.2 us -> 0 us
  between operations: 14.2 us -> 0.67 us
    psum x1 -> x0, waiting for transfers between devices: 249 us -> none  [on_device(): gram = lax.psum(local_gram, ('grp', 'dev'))]
    all_to_all x1 -> x0, local copies, waits for them, and re-layouts: 50.4 us -> none  [on_device(): lax.all_to_all(field, 'dev', split_axis=1, concat_axis=0, tiled=True)]
    reshape x1, local copies, waits for them, and re-layouts: 48.3 us -> 2.76 us  [on_device(): view = view.transpose(1, 0, 2, 4, 3).reshape(cols, rows, 8, LANES)]
    all_to_all x1 -> x4, blocking collectives: 109 us -> 146 us  [exchange(): return lax.all_to_all(x, axes, split_axis=0, concat_axis=0, tiled=True)]
    another operation x15 -> x0, other arithmetic: 36.2 us -> none  [the longest x9 19.6 us: on_device(): chol = jnp.linalg.cholesky(cross)]
    pallas_call x0 -> x3, Pallas kernels: none -> 33.5 us  [the longest x1 21.6 us: subspace(): pl.pallas_call(subspace_kernel, in_specs=[pl.BlockSpec(memory_space=pltpu...]
    dot_general x8 -> x0, matrix products: 25.2 us -> none  [product(): jnp.dot(left, right, precision=lax.Precision.HIGHEST, preferred_element_t...]
  transfers between devices with their start and end apart: 1 -> 2, of which waited for: 1 -> 2; matrix products, arithmetic and copies ran while one was open for 1% -> 0% of each run, Pallas kernels for 0% -> 0%
where the time goes in v1:
time: 192 us
  blocking collectives  146 us (76%)
  Pallas kernels  33.5 us (17%)
  starting transfers between devices  4.3 us (2%)
  local copies, waits for them, and re-layouts  3.51 us (2%)
  waiting for transfers between devices  3.19 us (2%)
    all_to_all x4, blocking collectives, exchange(): return lax.all_to_all(x, axes, split_axis=0, concat_axis=0, tiled=True)  146 us
    pallas_call x1, Pallas kernels, subspace(): pl.pallas_call(subspace_kernel, in_specs=[pl.BlockSpec(memory_space=pltpu...  21.6 us
    pallas_call x1, Pallas kernels, local_gram(): pl.pallas_call(gram_kernel, grid=(2,), in_specs=[pl.BlockSpec((64, None,...  6.61 us
    pallas_call x1, Pallas kernels, project(): pl.pallas_call(core_kernel, grid=(2,), in_specs=[pl.BlockSpec((rank, 512)...  5.28 us
    ppermute x1, starting transfers between devices, sum_over_devices(): other = lax.ppermute(mine, 'c', swap)  3.9 us
  transfers between devices with their start and end apart: 2, of which 2 were waited for; matrix products, arithmetic and copies ran while one was open for 0% of the time, Pallas kernels for 0%

profile of v1, /device:TPU:1, one launch (start us, length us, event | category | flops | bytes accessed | tf_op | source)
XLA Modules:
  0.0 191.9 jit_solution(4258571271989800550)
XLA Ops:
  0.6 2.8 %copy.6 = f32[128,8,8,128]{3,2,1,0:T(8,128)S(1)} copy(f32[128,8,8,128]{3,2,0,1:T(8,128)} %bitcast.19) | data formatting | bytes 8388608 | tf_op jit(solution)/shard_map/reshape | solution.py:181
  3.4 109.0 %all_to_all.20 = f32[128,8,8,128]{3,2,1,0:T(8,128)} all-to-all(f32[128,8,8,128]{3,2,1,0:T(8,128)S(1)} %copy.6), channel_id=1, replica_groups=mesh['y'=4,'x'=4,'z'=8,'c'=2] {'x','z','c'}, dimensions={0} | all-to-all | bytes 8388608 | tf_op jit(solution)/shard_map/all_to_all | solution.py:158
  112.4 6.6 %local_gram.1 = f32[10,128,128]{2,1,0:T(8,128)} custom-call(f32[64,2,64,128]{3,2,1,0:T(8,128)} %bitcast.17), custom_call_target="tpu_custom_call" | custom-call | tf_op jit(solution)/shard_map/local_gram/pallas_call | solution.py:63
  119.0 0.4 collective-permute-start
  119.4 1.9 %collective-permute-done = f32[2,640,128]{2,1,0:T(8,128)S(1)} collective-permute-done((f32[2,640,128]{2,1,0:T(8,128)}, f32[2,640,128]{2,1,0:T(8,128)S(1)}, u32[]{:S(2)}, u32[]{:S(2)}) %collective-permute-start) | collective-permute-done | bytes 655392 | tf_op jit(solution)/shard_map/ppermute | solution.py:165
  121.4 1.0 dynamic-slice_add_fusion
  122.4 15.5 %all_to_all.21 = f32[16,40,128]{2,1,0:T(8,128)S(1)} all-to-all(f32[16,40,128]{2,1,0:T(8,128)S(1)} %bitcast.24), channel_id=1, replica_groups=mesh['y'=4,'x'=4,'z'=8,'c'=2] {'y','x'}, dimensions={0} | all-to-all | bytes 655360 | tf_op jit(solution)/shard_map/all_to_all | solution.py:158
  137.9 10.4 %all_to_all.22 = f32[8,40,128]{2,1,0:T(8,128)S(1)} all-to-all(f32[8,40,128]{2,1,0:T(8,128)S(1)} %broadcast_in_dim.4), channel_id=1, replica_groups=mesh['y'=4,'x'=4,'z'=8,'c'=2] {'z'}, dimensions={0} | all-to-all | bytes 327680 | tf_op jit(solution)/shard_map/all_to_all | solution.py:158
  148.4 10.7 %all_to_all.23 = f32[16,40,128]{2,1,0:T(8,128)S(1)} all-to-all(f32[16,40,128]{2,1,0:T(8,128)S(1)} %broadcast_in_dim.5), channel_id=1, replica_groups=mesh['y'=4,'x'=4,'z'=8,'c'=2] {'y','x'}, dimensions={0} | all-to-all | bytes 655360 | tf_op jit(solution)/shard_map/all_to_all | solution.py:158
  159.1 0.0 copy-start
  159.1 3.9 %collective-permute-start.1 = (f32[5,128,128]{2,1,0:T(8,128)S(1)}, f32[5,128,128]{2,1,0:T(8,128)S(1)}, u32[]{:S(2)}, u32[]{:S(2)}) collective-permute-start(f32[5,128,128]{2,1,0:T(8,128)S(1)} %bitcast.22), channel_id=1, source_target_pairs={{0,1},{1,0},{2,3},{3,2},{4,5},{5,4},{6,7},{7,6},{8,9},{9,8},{10,11... | collective-permute-start | bytes 983048 | tf_op jit(solution)/shard_map/ppermute | solution.py:173
  163.0 1.3 collective-permute-done.1.other_ref
  164.3 0.0 copy-start.1
  164.3 0.0 copy-done
  164.3 0.7 copy-done.1
  165.0 21.6 %subspace.1.basis_ref = f32[64,512]{1,0:T(8,128)} custom-call(s32[1]{0:T(128)} %bitcast.core_ref, f32[5,128,128]{2,1,0:T(8,128)} %bitcast.23, f32[5,128,128]{2,1,0:T(8,128)} %copy-done.1, f32[64,512]{1,0:T(8,128)} %bitcast.27), custom_call_target="tpu_custom_call" | custom-call | tf_op jit(solution)/shard_map/subspace/pallas_call | solution.py:120
  186.6 5.3 %project.1 = f32[64,2,8,128]{3,2,1,0:T(8,128)} custom-call(f32[64,512]{1,0:T(8,128)} %subspace.1.basis_ref, f32[64,2,64,128]{3,2,1,0:T(8,128)} %bitcast.18), custom_call_target="tpu_custom_call" | custom-call | tf_op jit(solution)/shard_map/project/pallas_call | solution.py:144
  (4 shorter events, 0.1 us)
Async XLA Ops:
  119.0 2.3 %collective-permute-start = (f32[2,640,128]{2,1,0:T(8,128)}, f32[2,640,128]{2,1,0:T(8,128)S(1)}, u32[]{:S(2)}, u32[]{:S(2)}) collective-permute-start(f32[2,640,128]{2,1,0:T(8,128)} %bitcast.20), channel_id=1, source_target_pairs={{0,1},{1,0},{2,3},{3,2},{4,5},{5,4},{6,7},{7,6},{8,9},{9,8},{10,11... | collective-permute-start | bytes 1966088 | tf_op jit(solution)/shard_map/ppermute | solution.py:165
  159.1 5.2 %copy-start = (f32[16,40,128]{2,1,0:T(8,128)}, f32[16,40,128]{2,1,0:T(8,128)S(1)}, u32[]{:S(2)}) copy-start(f32[16,40,128]{2,1,0:T(8,128)S(1)} %all_to_all.23) | copy-start | bytes 983044
  159.1 5.2 %collective-permute-start.1 = (f32[5,128,128]{2,1,0:T(8,128)S(1)}, f32[5,128,128]{2,1,0:T(8,128)S(1)}, u32[]{:S(2)}, u32[]{:S(2)}) collective-permute-start(f32[5,128,128]{2,1,0:T(8,128)S(1)} %bitcast.22), channel_id=1, source_target_pairs={{0,1},{1,0},{2,3},{3,2},{4,5},{5,4},{6,7},{7,6},{8,9},{9,8},{10,11... | collective-permute-start | bytes 983048 | tf_op jit(solution)/shard_map/ppermute | solution.py:173
  164.3 0.7 copy-start.1

commit v2 on v1

--- a/solution.py
+++ b/solution.py
@@ -73,67 +73,87 @@
 
 def inverse_cholesky(cross):
     n = cross.shape[0]
+    blocks = n // 8
     row_id = lax.broadcasted_iota(jnp.int32, (n, n), 0)
     col_id = lax.broadcasted_iota(jnp.int32, (n, n), 1)
     work = jnp.concatenate([cross, (row_id == col_id).astype(jnp.float32)], axis=1)
-    rows = lax.broadcasted_iota(jnp.int32, (n, 2 * n), 0)
+    rows = [work[8 * i:8 * i + 8] for i in range(blocks)]
+    place = lax.broadcasted_iota(jnp.int32, (8, 2 * n), 0)
+
+    def spread(x):
+        return jnp.broadcast_to(x, (8, 2 * n))
+
     out = []
-    for k in range(0, n, 2):
-        first, second = work[k:k + 1, :], work[k + 1:k + 2, :]
-        a, b, c = first[:, k:k + 1], first[:, k + 1:k + 2], second[:, k + 1:k + 2]
-        ratio = b / a
-        rest = c - b * ratio
-        second = second - ratio * first
-        out.append(first / jnp.sqrt(a))
-        out.append(second / jnp.sqrt(rest))
-        if k + 2 < n:
-            base = (k + 2) // 8 * 8
-            tail = work[base:, :]
-            one = tail[:, k:k + 1]
-            two = tail[:, k + 1:k + 2] - ratio * one
-            update = tail - (one / a) * first - (two / rest) * second
-            tail = jnp.where(rows[base:, :] > k + 1, update, tail)
-            work = tail if base == 0 else jnp.concatenate([work[:base], tail], axis=0)
+    for b in range(blocks):
+        cols = {
+            i: [spread(rows[i][:, 8 * b + j:8 * b + j + 1]) for j in range(8)]
+            for i in range(b, blocks)
+        }
+        scale = jnp.zeros((8, 2 * n), jnp.float32)
+        for k in range(8):
+            pivot = spread(cols[b][k][k:k + 1])
+            inverse = 1.0 / pivot
+            root = lax.rsqrt(pivot)
+            root = root * (1.5 - 0.5 * pivot * root * root)
+            scale = jnp.where(place == k, root, scale)
+            row = spread(rows[b][k:k + 1])
+            entries = [spread(cols[b][j][k:k + 1]) for j in range(8)]
+            for i in range(b, blocks):
+                factor = cols[i][k] * inverse
+                if i == b:
+                    factor = jnp.where(place > k, factor, 0.0)
+                rows[i] = rows[i] - factor * row
+                for j in range(k + 1, 8):
+                    cols[i][j] = cols[i][j] - factor * entries[j]
+        out.append(rows[b] * scale)
     return jnp.concatenate(out, axis=0)[:, n:]
 
 
-def subspace_kernel(core_ref, mine_ref, other_ref, start_ref, out_ref, packed, gram):
-    core = core_ref[0]
-    packed[core] = mine_ref[...]
-    packed[1 - core] = other_ref[...]
+def swap_order(x, outer, inner):
+    return jnp.concatenate(
+        [
+            x[:, (o * inner + i) * 16:(o * inner + i + 1) * 16]
+            for i in range(inner) for o in range(outer)
+        ],
+        axis=1,
+    )
+
+
+def subspace_kernel(packed_ref, start_ref, factor_ref, basis_ref, gram):
     for n, (i, j) in enumerate(PACK):
-        block = packed[n // 5, n % 5]
+        block = packed_ref[n]
         gram[i * LANES:(i + 1) * LANES, j * LANES:(j + 1) * LANES] = block
         if i != j:
             gram[j * LANES:(j + 1) * LANES, i * LANES:(i + 1) * LANES] = block.T
-    basis = start_ref[...]
+    basis = swap_order(start_ref[...], 4, 8)
     for _ in range(ITERS):
         image = dot_nn(basis, gram[...], HIGHEST)
         image = image * lax.rsqrt(jnp.sum(image * image, axis=1, keepdims=True))
         cross = dot_nt(image, image, HIGHEST)
         basis = dot_nn(inverse_cholesky(cross), image, HIGHEST)
-    out_ref[...] = basis
-
-
-def subspace(core, mine, other, start):
+    basis_ref[...] = basis
+    factor_ref[...] = swap_order(basis, 8, 4)
+
+
+def subspace(packed, start):
     whole = pl.BlockSpec(memory_space=VMEM)
+    shape = jax.ShapeDtypeStruct(start.shape, jnp.float32)
     return pl.pallas_call(
         subspace_kernel,
-        in_specs=[pl.BlockSpec(memory_space=pltpu.SMEM), whole, whole, whole],
-        out_specs=whole,
-        out_shape=jax.ShapeDtypeStruct(start.shape, jnp.float32),
-        scratch_shapes=[
-            VMEM((2, 5, LANES, LANES), jnp.float32),
-            VMEM((512, 512), jnp.float32),
-        ],
+        in_specs=[whole, whole],
+        out_specs=(whole, whole),
+        out_shape=(shape, shape),
+        scratch_shapes=[VMEM((512, 512), jnp.float32)],
         name="subspace",
-    )(core, mine, other, start)
+    )(packed, start)
 
 
 def core_kernel(basis_ref, x_ref, out_ref):
-    x = gather_columns(x_ref, 512)
-    core = dot_nn(basis_ref[...], x, HIGHEST)
-    rank = core.shape[0]
+    both = jnp.concatenate(split(basis_ref[...]), axis=0)
+    high, mid = split(gather_columns(x_ref, 512))
+    core = dot_nn(both, high) + dot_nn(both, mid)
+    rank = basis_ref.shape[0]
+    core = core[:rank] + core[rank:]
     flat = out_ref.reshape(rank * 8, LANES)
     for c in range(8):
         flat[pl.ds(c, rank, stride=8), :] = core[:, c * LANES:(c + 1) * LANES]
@@ -159,35 +179,32 @@
 
 
 def sum_over_devices(packed):
-    swap = [(0, 1), (1, 0)]
     core = lax.axis_index("c")
     flat = packed.reshape(2, 640, LANES)
-    theirs = lax.ppermute(flat, "c", swap)
+    theirs = lax.ppermute(flat, "c", [(0, 1), (1, 0)])
     half = lax.dynamic_index_in_dim(flat, core, 0, False) + lax.dynamic_index_in_dim(theirs, core, 0, False)
     parts = exchange(half.reshape(16, 40, LANES), ("y", "x"))
     part = jnp.sum(parts, axis=0)
     parts = exchange(jnp.broadcast_to(part[None], (8, 40, LANES)), "z")
     part = jnp.sum(parts, axis=0)
-    half = exchange(jnp.broadcast_to(part[None], (16, 40, LANES)), ("y", "x"))
-    mine = half.reshape(5, LANES, LANES)
-    other = lax.ppermute(mine, "c", swap)
-    return core, mine, other
+    whole = exchange(jnp.broadcast_to(part[None], (32, 40, LANES)), ("c", "y", "x"))
+    return whole.reshape(len(PACK), LANES, LANES)
 
 
 def on_device(field, start_basis):
     rows, cols = field.shape[0], field.shape[1]
     view = field.reshape(rows, cols, 2, LANES, 4)
     view = with_layout_constraint(view, Layout(major_to_minor=(0, 1, 2, 4, 3)))
-    view = view.transpose(1, 0, 2, 4, 3).reshape(cols, rows, 8, LANES)
-    moved = exchange(view, ("x", "z", "c"))
+    view = view.transpose(1, 0, 2, 4, 3).reshape(4, 8, cols // 32, rows, 8, LANES)
+    view = view.transpose(1, 0, 2, 3, 4, 5).reshape(cols, rows, 8, LANES)
+    moved = exchange(view, ("z", "x", "c"))
     blocks = moved.reshape(64, cols // 64, rows * 8, LANES)
-    packed = local_gram(blocks)
-    core, mine, other = sum_over_devices(packed)
-    basis = subspace(core.reshape(1), mine, other, start_basis.T)
+    packed = sum_over_devices(local_gram(blocks))
+    factor, basis = subspace(packed, start_basis.T)
     out = project(basis, blocks)
     rank = basis.shape[0]
     out = out.reshape(rank, cols // 64, 2, 4, LANES).transpose(0, 1, 2, 4, 3)
-    return basis.T, out.reshape(rank, cols // 64, 256, 4)
+    return factor.T, out.reshape(rank, cols // 64, 256, 4)
 
 
 def solution(mesh):

time: 192 us -> 182 us (0.948)
  Pallas kernels: 33.5 us -> 21.5 us
  blocking collectives: 146 us -> 152 us
  starting transfers between devices: 4.3 us -> 2.09 us
    pallas_call x1, Pallas kernels: 21.6 us -> 11.2 us  [subspace(): pl.pallas_call(subspace_kernel, in_specs=[whole, whole], out_specs=(whole...]
    all_to_all x4, blocking collectives: 146 us -> 152 us  [exchange(): return lax.all_to_all(x, axes, split_axis=0, concat_axis=0, tiled=True)]
    reshape x1 -> x0, local copies, waits for them, and re-layouts: 2.76 us -> none  [on_device(): view = view.transpose(1, 0, 2, 4, 3).reshape(cols, rows, 8, LANES)]
    transpose x0 -> x1, local copies, waits for them, and re-layouts: none -> 2.76 us  [on_device(): view = view.transpose(1, 0, 2, 3, 4, 5).reshape(cols, rows, 8, LANES)]
    ppermute x2 -> x1, starting transfers between devices: 4.3 us -> 2.09 us  [sum_over_devices(): theirs = lax.ppermute(flat, 'c', [(0, 1), (1, 0)])]
  transfers between devices with their start and end apart: 2 -> 1, of which waited for: 2 -> 1; matrix products, arithmetic and copies ran while one was open for 0% -> 0% of each run, Pallas kernels for 0% -> 0%
where the time goes in v2:
time: 182 us
  blocking collectives  152 us (84%)
  Pallas kernels  21.5 us (12%)
  local copies, waits for them, and re-layouts  2.81 us (2%)
  starting transfers between devices  2.09 us (1%)
  waiting for transfers between devices  1.93 us (1%)
    all_to_all x4, blocking collectives, exchange(): return lax.all_to_all(x, axes, split_axis=0, concat_axis=0, tiled=True)  152 us
    pallas_call x1, Pallas kernels, subspace(): pl.pallas_call(subspace_kernel, in_specs=[whole, whole], out_specs=(whole...  11.2 us
    pallas_call x1, Pallas kernels, local_gram(): pl.pallas_call(gram_kernel, grid=(2,), in_specs=[pl.BlockSpec((64, None,...  6.61 us
    pallas_call x1, Pallas kernels, project(): pl.pallas_call(core_kernel, grid=(2,), in_specs=[pl.BlockSpec((rank, 512)...  3.68 us
  transfers between devices with their start and end apart: 1, of which 1 were waited for; matrix products, arithmetic and copies ran while one was open for 0% of the time, Pallas kernels for 0%

profile of v2, /device:TPU:1, one launch (start us, length us, event | category | flops | bytes accessed | tf_op | source)
XLA Modules:
  0.0 182.0 jit_solution(1048610220974058841)
XLA Ops:
  0.6 2.8 %copy.6 = f32[8,4,4,8,8,128]{5,4,3,2,1,0:T(8,128)S(1)} copy(f32[8,4,4,8,8,128]{5,4,2,0,1,3:T(8,128)} %bitcast.22) | data formatting | bytes 8388608 | tf_op jit(solution)/shard_map/transpose | solution.py:199
  3.4 107.5 %all_to_all.20 = f32[128,8,8,128]{3,2,1,0:T(8,128)} all-to-all(f32[128,8,8,128]{3,2,1,0:T(8,128)S(1)} %bitcast.21), channel_id=1, replica_groups=mesh['y'=4,'x'=4,'z'=8,'c'=2] {'z','x','c'}, dimensions={0} | all-to-all | bytes 8388608 | tf_op jit(solution)/shard_map/all_to_all | solution.py:178
  110.9 6.6 %local_gram.1 = f32[10,128,128]{2,1,0:T(8,128)} custom-call(f32[64,2,64,128]{3,2,1,0:T(8,128)} %bitcast.19), custom_call_target="tpu_custom_call" | custom-call | tf_op jit(solution)/shard_map/local_gram/pallas_call | solution.py:63
  117.5 2.1 %collective-permute-start = (f32[2,640,128]{2,1,0:T(8,128)}, f32[2,640,128]{2,1,0:T(8,128)S(1)}, u32[]{:S(2)}, u32[]{:S(2)}) collective-permute-start(f32[2,640,128]{2,1,0:T(8,128)} %bitcast.24), channel_id=1, source_target_pairs={{0,1},{1,0},{2,3},{3,2},{4,5},{5,4},{6,7},{7,6},{8,9},{9,8},{10,11... | collective-permute-start | bytes 1966088 | tf_op jit(solution)/shard_map/ppermute | solution.py:184
  119.6 1.9 %collective-permute-done = f32[2,640,128]{2,1,0:T(8,128)S(1)} collective-permute-done((f32[2,640,128]{2,1,0:T(8,128)}, f32[2,640,128]{2,1,0:T(8,128)S(1)}, u32[]{:S(2)}, u32[]{:S(2)}) %collective-permute-start) | collective-permute-done | bytes 655392 | tf_op jit(solution)/shard_map/ppermute | solution.py:184
  121.6 1.0 dynamic-slice_add_fusion
  122.6 15.3 %all_to_all.21 = f32[16,40,128]{2,1,0:T(8,128)S(1)} all-to-all(f32[16,40,128]{2,1,0:T(8,128)S(1)} %bitcast.26), channel_id=1, replica_groups=mesh['y'=4,'x'=4,'z'=8,'c'=2] {'y','x'}, dimensions={0} | all-to-all | bytes 655360 | tf_op jit(solution)/shard_map/all_to_all | solution.py:178
  138.0 10.8 %all_to_all.22 = f32[8,40,128]{2,1,0:T(8,128)S(1)} all-to-all(f32[8,40,128]{2,1,0:T(8,128)S(1)} %broadcast_in_dim.4), channel_id=1, replica_groups=mesh['y'=4,'x'=4,'z'=8,'c'=2] {'z'}, dimensions={0} | all-to-all | bytes 327680 | tf_op jit(solution)/shard_map/all_to_all | solution.py:178
  148.8 18.3 %all_to_all.23 = f32[32,40,128]{2,1,0:T(8,128)} all-to-all(f32[32,40,128]{2,1,0:T(8,128)S(1)} %broadcast_in_dim.5), channel_id=1, replica_groups=mesh['y'=4,'x'=4,'z'=8,'c'=2] {'c','y','x'}, dimensions={0} | all-to-all | bytes 1310720 | tf_op jit(solution)/shard_map/all_to_all | solution.py:178
  167.1 11.2 %subspace.1 = (f32[64,512]{1,0:T(8,128)}, f32[64,512]{1,0:T(8,128)}) custom-call(f32[10,128,128]{2,1,0:T(8,128)} %bitcast.23, f32[64,512]{1,0:T(8,128)} %bitcast.28), custom_call_target="tpu_custom_call" | custom-call | tf_op jit(solution)/shard_map/subspace/pallas_call | solution.py:141
  178.3 3.7 %project.1 = f32[64,2,8,128]{3,2,1,0:T(8,128)} custom-call(f32[64,512]{1,0:T(8,128)} %get-tuple-element.5.basis_ref, f32[64,2,64,128]{3,2,1,0:T(8,128)} %bitcast.20), custom_call_target="tpu_custom_call" | custom-call | tf_op jit(solution)/shard_map/project/pallas_call | solution.py:164
  (4 shorter events, 0.1 us)
Async XLA Ops:
  117.5 4.0 %collective-permute-start = (f32[2,640,128]{2,1,0:T(8,128)}, f32[2,640,128]{2,1,0:T(8,128)S(1)}, u32[]{:S(2)}, u32[]{:S(2)}) collective-permute-start(f32[2,640,128]{2,1,0:T(8,128)} %bitcast.24), channel_id=1, source_target_pairs={{0,1},{1,0},{2,3},{3,2},{4,5},{5,4},{6,7},{7,6},{8,9},{9,8},{10,11... | collective-permute-start | bytes 1966088 | tf_op jit(solution)/shard_map/ppermute | solution.py:184

commit v3 on v2

--- a/solution.py
+++ b/solution.py
@@ -8,8 +8,10 @@
 
 ITERS = 3
 LANES = 128
+KERNEL_VMEM = 40 * 1024 * 1024
 PACK = tuple((i, j) for i in range(4) for j in range(i, 4))
 VMEM = pltpu.VMEM
+WHOLE = pl.BlockSpec(memory_space=VMEM)
 HIGHEST = lax.Precision.HIGHEST
 
 
@@ -27,9 +29,13 @@
     )
 
 
-def gather_columns(x_ref, rows):
+def gather_columns(x_ref):
     return jnp.concatenate(
-        [x_ref[:, pl.ds(c, 8, stride=8), :].reshape(rows, LANES) for c in range(8)], axis=1
+        [
+            x_ref[:, part, pl.ds(c, 8, stride=8), :].reshape(512, LANES)
+            for part in range(2) for c in range(8)
+        ],
+        axis=1,
     )
 
 
@@ -39,36 +45,41 @@
     return high, mid
 
 
-def gram_kernel(x_ref, packed_ref, square, mixed):
-    step = pl.program_id(0)
-    x = gather_columns(x_ref, 512)
-    high, mid = split(x)
-    square_step = dot_nt(high, high)
-    mixed_step = dot_nt(high, mid) + 0.5 * dot_nt(mid, mid)
-
-    @pl.when(step == 0)
-    def _():
-        square[...] = square_step
-        mixed[...] = mixed_step
-
-    @pl.when(step == pl.num_programs(0) - 1)
-    def _():
-        both = mixed[...] + mixed_step
-        whole = square[...] + square_step + both + both.T
-        for n, (i, j) in enumerate(PACK):
-            packed_ref[n] = whole[i * LANES:(i + 1) * LANES, j * LANES:(j + 1) * LANES]
+def gram_kernel(x_ref, packed_ref, pieces_ref, pieces, sems):
+    high, mid = split(gather_columns(x_ref))
+    pieces[0] = high
+    pieces[1] = mid
+    copies = [
+        pltpu.make_async_copy(pieces.at[n], pieces_ref.at[n], sems.at[n]) for n in range(2)
+    ]
+    for copy in copies:
+        copy.start()
+    square = dot_nt(high, high)
+    mixed = dot_nt(high, mid) + 0.5 * dot_nt(mid, mid)
+    for n, (i, j) in enumerate(PACK):
+        row, col = slice(i * LANES, (i + 1) * LANES), slice(j * LANES, (j + 1) * LANES)
+        packed_ref[n] = square[row, col] + mixed[row, col] + mixed[col, row].T
+    for copy in copies:
+        copy.wait()
+
+
+def on_chip(x):
+    return pltpu.with_memory_space_constraint(x, VMEM)
 
 
 def local_gram(blocks):
     return pl.pallas_call(
         gram_kernel,
-        grid=(2,),
-        in_specs=[pl.BlockSpec((64, None, 64, LANES), lambda i: (0, i, 0, 0))],
-        out_specs=pl.BlockSpec((len(PACK), LANES, LANES), lambda i: (0, 0, 0)),
-        out_shape=jax.ShapeDtypeStruct((len(PACK), LANES, LANES), jnp.float32),
-        scratch_shapes=[VMEM((512, 512), jnp.float32), VMEM((512, 512), jnp.float32)],
+        in_specs=[WHOLE],
+        out_specs=(WHOLE, pl.BlockSpec(memory_space=pltpu.HBM)),
+        out_shape=(
+            VMEM((len(PACK), LANES, LANES), jnp.float32),
+            pltpu.HBM((2, 512, 2048), jnp.bfloat16),
+        ),
+        scratch_shapes=[VMEM((2, 512, 2048), jnp.bfloat16), pltpu.SemaphoreType.DMA((2,))],
+        compiler_params=pltpu.CompilerParams(vmem_limit_bytes=KERNEL_VMEM),
         name="local_gram",
-    )(blocks)
+    )(on_chip(blocks))
 
 
 def inverse_cholesky(cross):
@@ -119,59 +130,70 @@
     )
 
 
-def subspace_kernel(packed_ref, start_ref, factor_ref, basis_ref, gram):
+def finish_kernel(
+    core_ref, mine_ref, other_ref, start_ref, pieces_ref, factor_ref, out_ref,
+    packed, gram, basis_ref, pieces, sems,
+):
+    copies = [
+        pltpu.make_async_copy(pieces_ref.at[n], pieces.at[n], sems.at[n]) for n in range(2)
+    ]
+    for copy in copies:
+        copy.start()
+    core = core_ref[0]
+    packed[core] = mine_ref[...]
+    packed[1 - core] = other_ref[...]
     for n, (i, j) in enumerate(PACK):
-        block = packed_ref[n]
+        block = packed[n // 5, n % 5]
         gram[i * LANES:(i + 1) * LANES, j * LANES:(j + 1) * LANES] = block
         if i != j:
             gram[j * LANES:(j + 1) * LANES, i * LANES:(i + 1) * LANES] = block.T
-    basis = swap_order(start_ref[...], 4, 8)
-    for _ in range(ITERS):
-        image = dot_nn(basis, gram[...], HIGHEST)
+    basis_ref[...] = swap_order(start_ref[...], 4, 8)
+
+    def iterate(_, carry):
+        image = dot_nn(basis_ref[...], gram[...], HIGHEST)
         image = image * lax.rsqrt(jnp.sum(image * image, axis=1, keepdims=True))
         cross = dot_nt(image, image, HIGHEST)
-        basis = dot_nn(inverse_cholesky(cross), image, HIGHEST)
-    basis_ref[...] = basis
+        basis_ref[...] = dot_nn(inverse_cholesky(cross), image, HIGHEST)
+        return carry
+
+    lax.fori_loop(0, ITERS, iterate, 0)
+    basis = basis_ref[...]
     factor_ref[...] = swap_order(basis, 8, 4)
 
-
-def subspace(packed, start):
-    whole = pl.BlockSpec(memory_space=VMEM)
-    shape = jax.ShapeDtypeStruct(start.shape, jnp.float32)
+    rank = basis.shape[0]
+    both = jnp.concatenate(split(basis), axis=0)
+    for copy in copies:
+        copy.wait()
+    product = dot_nn(both, pieces[0]) + dot_nn(both, pieces[1])
+    product = product[:rank] + product[rank:]
+    flat = out_ref.reshape(rank * 16, LANES)
+    for c in range(16):
+        flat[pl.ds(c, rank, stride=16), :] = product[:, c * LANES:(c + 1) * LANES]
+
+
+def finish(core, mine, other, start, pieces):
+    rank = start.shape[0]
     return pl.pallas_call(
-        subspace_kernel,
-        in_specs=[whole, whole],
-        out_specs=(whole, whole),
-        out_shape=(shape, shape),
-        scratch_shapes=[VMEM((512, 512), jnp.float32)],
-        name="subspace",
-    )(packed, start)
-
-
-def core_kernel(basis_ref, x_ref, out_ref):
-    both = jnp.concatenate(split(basis_ref[...]), axis=0)
-    high, mid = split(gather_columns(x_ref, 512))
-    core = dot_nn(both, high) + dot_nn(both, mid)
-    rank = basis_ref.shape[0]
-    core = core[:rank] + core[rank:]
-    flat = out_ref.reshape(rank * 8, LANES)
-    for c in range(8):
-        flat[pl.ds(c, rank, stride=8), :] = core[:, c * LANES:(c + 1) * LANES]
-
-
-def project(basis, blocks):
-    rank = basis.shape[0]
-    return pl.pallas_call(
-        core_kernel,
-        grid=(2,),
+        finish_kernel,
         in_specs=[
-            pl.BlockSpec((rank, 512), lambda i: (0, 0)),
-            pl.BlockSpec((64, None, 64, LANES), lambda i: (0, i, 0, 0)),
-        ],
-        out_specs=pl.BlockSpec((rank, None, 8, LANES), lambda i: (0, i, 0, 0)),
-        out_shape=jax.ShapeDtypeStruct((rank, 2, 8, LANES), jnp.float32),
-        name="project",
-    )(basis, blocks)
+            pl.BlockSpec(memory_space=pltpu.SMEM), WHOLE, WHOLE, WHOLE,
+            pl.BlockSpec(memory_space=pltpu.HBM),
+        ],
+        out_specs=(WHOLE, WHOLE),
+        out_shape=(
+            jax.ShapeDtypeStruct(start.shape, jnp.float32),
+            jax.ShapeDtypeStruct((rank, 2, 8, LANES), jnp.float32),
+        ),
+        scratch_shapes=[
+            VMEM((2, 5, LANES, LANES), jnp.float32),
+            VMEM((512, 512), jnp.float32),
+            VMEM(start.shape, jnp.float32),
+            VMEM((2, 512, 2048), jnp.bfloat16),
+            pltpu.SemaphoreType.DMA((2,)),
+        ],
+        compiler_params=pltpu.CompilerParams(vmem_limit_bytes=KERNEL_VMEM),
+        name="finish",
+    )(core, on_chip(mine), on_chip(other), on_chip(start), pltpu.with_memory_space_constraint(pieces, pltpu.HBM))
 
 
 def exchange(x, axes):
@@ -187,8 +209,9 @@
     part = jnp.sum(parts, axis=0)
     parts = exchange(jnp.broadcast_to(part[None], (8, 40, LANES)), "z")
     part = jnp.sum(parts, axis=0)
-    whole = exchange(jnp.broadcast_to(part[None], (32, 40, LANES)), ("c", "y", "x"))
-    return whole.reshape(len(PACK), LANES, LANES)
+    half = exchange(jnp.broadcast_to(part[None], (16, 40, LANES)), ("y", "x"))
+    mine = half.reshape(5, LANES, LANES)
+    return core.reshape(1), mine, lax.ppermute(mine, "c", [(0, 1), (1, 0)])
 
 
 def on_device(field, start_basis):
@@ -199,10 +222,10 @@
     view = view.transpose(1, 0, 2, 3, 4, 5).reshape(cols, rows, 8, LANES)
     moved = exchange(view, ("z", "x", "c"))
     blocks = moved.reshape(64, cols // 64, rows * 8, LANES)
-    packed = sum_over_devices(local_gram(blocks))
-    factor, basis = subspace(packed, start_basis.T)
-    out = project(basis, blocks)
-    rank = basis.shape[0]
+    packed, pieces = local_gram(blocks)
+    core, mine, other = sum_over_devices(packed)
+    factor, out = finish(core, mine, other, start_basis.T, pieces)
+    rank = factor.shape[0]
     out = out.reshape(rank, cols // 64, 2, 4, LANES).transpose(0, 1, 2, 4, 3)
     return factor.T, out.reshape(rank, cols // 64, 256, 4)
 

time: 182 us -> 173 us (0.951)
  blocking collectives: 152 us -> 144 us
  Pallas kernels: 21.5 us -> 16.3 us
  starting transfers between devices: 2.09 us -> 6.07 us
    all_to_all x4, blocking collectives: 152 us -> 144 us  [exchange(): return lax.all_to_all(x, axes, split_axis=0, concat_axis=0, tiled=True)]
    pallas_call x3 -> x2, Pallas kernels: 21.5 us -> 16.3 us  [the longest x1 12.2 us: finish(): pl.pallas_call(finish_kernel, in_specs=[pl.BlockSpec(memory_space=pltpu.S...]
    ppermute x0 -> x1, starting transfers between devices: none -> 3.9 us  [sum_over_devices(): return (core.reshape(1), mine, lax.ppermute(mine, 'c', [(0, 1), (1, 0)]))]
  transfers between devices with their start and end apart: 1 -> 2, of which waited for: 1 -> 2; matrix products, arithmetic and copies ran while one was open for 0% -> 0% of each run, Pallas kernels for 0% -> 0%
where the time goes in v3:
time: 173 us
  blocking collectives  144 us (83%)
  Pallas kernels  16.3 us (9%)
  starting transfers between devices  6.07 us (4%)
  waiting for transfers between devices  2.98 us (2%)
  local copies, waits for them, and re-layouts  2.8 us (2%)
    all_to_all x4, blocking collectives, exchange(): return lax.all_to_all(x, axes, split_axis=0, concat_axis=0, tiled=True)  144 us
    pallas_call x1, Pallas kernels, finish(): pl.pallas_call(finish_kernel, in_specs=[pl.BlockSpec(memory_space=pltpu.S...  12.2 us
    pallas_call x1, Pallas kernels, local_gram(): pl.pallas_call(gram_kernel, in_specs=[WHOLE], out_specs=(WHOLE, pl.BlockS...  4.16 us
    ppermute x1, starting transfers between devices, sum_over_devices(): return (core.reshape(1), mine, lax.ppermute(mine, 'c', [(0, 1), (1, 0)]))  3.9 us
  transfers between devices with their start and end apart: 2, of which 2 were waited for; matrix products, arithmetic and copies ran while one was open for 0% of the time, Pallas kernels for 0%

profile of v3, /device:TPU:1, one launch (start us, length us, event | category | flops | bytes accessed | tf_op | source)
XLA Modules:
  0.0 173.0 jit_solution(12595982316605182522)
XLA Ops:
  0.6 2.8 %copy.6 = f32[8,4,4,8,8,128]{5,4,3,2,1,0:T(8,128)S(1)} copy(f32[8,4,4,8,8,128]{5,4,2,0,1,3:T(8,128)} %bitcast.27) | data formatting | bytes 8388608 | tf_op jit(solution)/shard_map/transpose | solution.py:222
  3.4 107.4 %all_to_all.20 = f32[128,8,8,128]{3,2,1,0:T(8,128)S(1)} all-to-all(f32[128,8,8,128]{3,2,1,0:T(8,128)S(1)} %bitcast.26), channel_id=1, replica_groups=mesh['y'=4,'x'=4,'z'=8,'c'=2] {'z','x','c'}, dimensions={0} | all-to-all | bytes 8388608 | tf_op jit(solution)/shard_map/all_to_all | solution.py:200
  110.8 0.0 copy-start
  110.8 4.2 %local_gram.1 = (f32[10,128,128]{2,1,0:T(8,128)S(1)}, bf16[2,512,2048]{2,1,0:T(8,128)(2,1)}) custom-call(f32[64,2,64,128]{3,2,1,0:T(8,128)S(1)} %bitcast.20), custom_call_target="tpu_custom_call" | custom-call | tf_op jit(solution)/shard_map/local_gram/pallas_call | solution.py:71
  115.0 2.2 %collective-permute-start = (f32[2,640,128]{2,1,0:T(8,128)S(1)}, f32[2,640,128]{2,1,0:T(8,128)S(1)}, u32[]{:S(2)}, u32[]{:S(2)}) collective-permute-start(f32[2,640,128]{2,1,0:T(8,128)S(1)} %bitcast.23), channel_id=1, source_target_pairs={{0,1},{1,0},{2,3},{3,2},{4,5},{5,4},{6,7},{7,6},{8,9},{9,8},{10,11... | collective-permute-start | bytes 1966088 | tf_op jit(solution)/shard_map/ppermute | solution.py:206
  117.2 1.7 collective-permute-done
  118.9 15.3 %all_to_all.21 = f32[16,40,128]{2,1,0:T(8,128)S(1)} all-to-all(f32[16,40,128]{2,1,0:T(8,128)S(1)} %bitcast.28), channel_id=1, replica_groups=mesh['y'=4,'x'=4,'z'=8,'c'=2] {'y','x'}, dimensions={0} | all-to-all | bytes 655360 | tf_op jit(solution)/shard_map/all_to_all | solution.py:200
  134.3 10.8 %all_to_all.22 = f32[8,40,128]{2,1,0:T(8,128)S(1)} all-to-all(f32[8,40,128]{2,1,0:T(8,128)S(1)} %broadcast_in_dim.4), channel_id=1, replica_groups=mesh['y'=4,'x'=4,'z'=8,'c'=2] {'z'}, dimensions={0} | all-to-all | bytes 327680 | tf_op jit(solution)/shard_map/all_to_all | solution.py:200
  145.1 10.6 %all_to_all.23 = f32[16,40,128]{2,1,0:T(8,128)S(1)} all-to-all(f32[16,40,128]{2,1,0:T(8,128)S(1)} %broadcast_in_dim.5), channel_id=1, replica_groups=mesh['y'=4,'x'=4,'z'=8,'c'=2] {'y','x'}, dimensions={0} | all-to-all | bytes 655360 | tf_op jit(solution)/shard_map/all_to_all | solution.py:200
  155.7 3.9 %collective-permute-start.1 = (f32[5,128,128]{2,1,0:T(8,128)S(1)}, f32[5,128,128]{2,1,0:T(8,128)S(1)}, u32[]{:S(2)}, u32[]{:S(2)}) collective-permute-start(f32[5,128,128]{2,1,0:T(8,128)S(1)} %bitcast.21), channel_id=1, source_target_pairs={{0,1},{1,0},{2,3},{3,2},{4,5},{5,4},{6,7},{7,6},{8,9},{9,8},{10,11... | collective-permute-start | bytes 983048 | tf_op jit(solution)/shard_map/ppermute | solution.py:214
  159.6 1.3 collective-permute-done.1.other_ref
  160.9 0.0 copy-done
  160.9 12.2 %finish.1 = (f32[64,512]{1,0:T(8,128)}, f32[64,2,8,128]{3,2,1,0:T(8,128)}) custom-call(s32[1]{0:T(128)} %bitcast.core_ref, f32[5,128,128]{2,1,0:T(8,128)S(1)} %bitcast.22, f32[5,128,128]{2,1,0:T(8,128)S(1)} %collective-permute-done.1.other_ref, f32[64,512]{1,0:T(8,128)S(1)} %bitcast.25, bf16[2,512,2048]{2,1,0:T(8,128)(2,1)} %get-tuple-element.7.pieces_ref), custom_call_target="tpu_custom_call" | custom-call | tf_op jit(solution)/shard_map/finish/pallas_call | solution.py:176
  (5 shorter events, 0.1 us)
Async XLA Ops:
  110.8 50.1 %copy-start = (f32[512,64]{0,1:T(8,128)S(1)}, f32[512,64]{0,1:T(8,128)}, u32[]{:S(2)}) copy-start(f32[512,64]{0,1:T(8,128)} %param.3) | copy-start | bytes 393220
  115.0 3.9 %collective-permute-start = (f32[2,640,128]{2,1,0:T(8,128)S(1)}, f32[2,640,128]{2,1,0:T(8,128)S(1)}, u32[]{:S(2)}, u32[]{:S(2)}) collective-permute-start(f32[2,640,128]{2,1,0:T(8,128)S(1)} %bitcast.23), channel_id=1, source_target_pairs={{0,1},{1,0},{2,3},{3,2},{4,5},{5,4},{6,7},{7,6},{8,9},{9,8},{10,11... | collective-permute-start | bytes 1966088 | tf_op jit(solution)/shard_map/ppermute | solution.py:206
  155.7 5.2 %collective-permute-start.1 = (f32[5,128,128]{2,1,0:T(8,128)S(1)}, f32[5,128,128]{2,1,0:T(8,128)S(1)}, u32[]{:S(2)}, u32[]{:S(2)}) collective-permute-start(f32[5,128,128]{2,1,0:T(8,128)S(1)} %bitcast.21), channel_id=1, source_target_pairs={{0,1},{1,0},{2,3},{3,2},{4,5},{5,4},{6,7},{7,6},{8,9},{9,8},{10,11... | collective-permute-start | bytes 983048 | tf_op jit(solution)/shard_map/ppermute | solution.py:214

commit v4 on v3

--- a/solution.py
+++ b/solution.py
@@ -45,6 +45,21 @@
     return high, mid
 
 
+def split_three(x):
+    high, mid = split(x)
+    low = (x - high.astype(jnp.float32) - mid.astype(jnp.float32)).astype(jnp.bfloat16)
+    return high, mid, low
+
+
+def product(left, right, dot):
+    high, mid, low = left
+    n = high.shape[0]
+    one = dot(jnp.concatenate([high, mid, low], axis=0), right[0])
+    two = dot(jnp.concatenate([high, mid], axis=0), right[1])
+    three = dot(high, right[2])
+    return one[:n] + (one[n:2 * n] + two[:n]) + (one[2 * n:] + two[n:] + three)
+
+
 def gram_kernel(x_ref, packed_ref, pieces_ref, pieces, sems):
     high, mid = split(gather_columns(x_ref))
     pieces[0] = high
@@ -54,8 +69,8 @@
     ]
     for copy in copies:
         copy.start()
+    mixed = dot_nt(jnp.concatenate([high, mid], axis=1), jnp.concatenate([mid, mid * 0.5], axis=1))
     square = dot_nt(high, high)
-    mixed = dot_nt(high, mid) + 0.5 * dot_nt(mid, mid)
     for n, (i, j) in enumerate(PACK):
         row, col = slice(i * LANES, (i + 1) * LANES), slice(j * LANES, (j + 1) * LANES)
         packed_ref[n] = square[row, col] + mixed[row, col] + mixed[col, row].T
@@ -83,40 +98,46 @@
 
 
 def inverse_cholesky(cross):
-    n = cross.shape[0]
-    blocks = n // 8
+    n, width = cross.shape[0], 16
+    groups = n // 8
     row_id = lax.broadcasted_iota(jnp.int32, (n, n), 0)
     col_id = lax.broadcasted_iota(jnp.int32, (n, n), 1)
     work = jnp.concatenate([cross, (row_id == col_id).astype(jnp.float32)], axis=1)
-    rows = [work[8 * i:8 * i + 8] for i in range(blocks)]
+    rows = [work[8 * i:8 * i + 8] for i in range(groups)]
     place = lax.broadcasted_iota(jnp.int32, (8, 2 * n), 0)
 
     def spread(x):
         return jnp.broadcast_to(x, (8, 2 * n))
 
     out = []
-    for b in range(blocks):
+    for first in range(0, groups, width // 8):
         cols = {
-            i: [spread(rows[i][:, 8 * b + j:8 * b + j + 1]) for j in range(8)]
-            for i in range(b, blocks)
+            i: [spread(rows[i][:, 8 * first + j:8 * first + j + 1]) for j in range(width)]
+            for i in range(first, groups)
         }
-        scale = jnp.zeros((8, 2 * n), jnp.float32)
-        for k in range(8):
-            pivot = spread(cols[b][k][k:k + 1])
+        scales = [jnp.zeros((8, 2 * n), jnp.float32) for _ in range(width // 8)]
+        for k in range(width):
+            home, at = first + k // 8, k % 8
+            pivot = spread(cols[home][k][at:at + 1])
             inverse = 1.0 / pivot
             root = lax.rsqrt(pivot)
             root = root * (1.5 - 0.5 * pivot * root * root)
-            scale = jnp.where(place == k, root, scale)
-            row = spread(rows[b][k:k + 1])
-            entries = [spread(cols[b][j][k:k + 1]) for j in range(8)]
-            for i in range(b, blocks):
+            scales[k // 8] = jnp.where(place == at, root, scales[k // 8])
+            row = spread(rows[home][at:at + 1])
+            entries = {j: spread(cols[home][j][at:at + 1]) for j in range(k + 1, width)}
+            for i in range(home, groups):
                 factor = cols[i][k] * inverse
-                if i == b:
-                    factor = jnp.where(place > k, factor, 0.0)
-                rows[i] = rows[i] - factor * row
-                for j in range(k + 1, 8):
-                    cols[i][j] = cols[i][j] - factor * entries[j]
-        out.append(rows[b] * scale)
+                if i == home:
+                    if at == 7:
+                        continue
+                    rows[i] = rows[i] - jnp.where(place > at, factor, 0.0) * row
+                    for j, entry in entries.items():
+                        cols[i][j] = cols[i][j] - (cols[i][k] * entry) * inverse
+                else:
+                    rows[i] = rows[i] - factor * row
+                    for j, entry in entries.items():
+                        cols[i][j] = cols[i][j] - factor * entry
+        out.extend(rows[first + q] * scale for q, scale in enumerate(scales))
     return jnp.concatenate(out, axis=0)[:, n:]
 
 
@@ -144,31 +165,42 @@
     packed[1 - core] = other_ref[...]
     for n, (i, j) in enumerate(PACK):
         block = packed[n // 5, n % 5]
-        gram[i * LANES:(i + 1) * LANES, j * LANES:(j + 1) * LANES] = block
+        row, col = slice(i * LANES, (i + 1) * LANES), slice(j * LANES, (j + 1) * LANES)
+        for k, piece in enumerate(split_three(block)):
+            gram[k, row, col] = piece
         if i != j:
-            gram[j * LANES:(j + 1) * LANES, i * LANES:(i + 1) * LANES] = block.T
-    basis_ref[...] = swap_order(start_ref[...], 4, 8)
-
-    def iterate(_, carry):
-        image = dot_nn(basis_ref[...], gram[...], HIGHEST)
-        image = image * lax.rsqrt(jnp.sum(image * image, axis=1, keepdims=True))
-        cross = dot_nt(image, image, HIGHEST)
-        basis_ref[...] = dot_nn(inverse_cholesky(cross), image, HIGHEST)
+            for k, piece in enumerate(split_three(block.T)):
+                gram[k, col, row] = piece
+    diagonal = sum(packed[n // 5, n % 5] for n, (i, j) in enumerate(PACK) if i == j)
+    row_id = lax.broadcasted_iota(jnp.int32, (LANES, LANES), 0)
+    col_id = lax.broadcasted_iota(jnp.int32, (LANES, LANES), 1)
+    trace = jnp.sum(jnp.where(row_id == col_id, diagonal, 0.0), axis=0, keepdims=True)
+    scale = 512.0 / jnp.sum(trace, axis=1, keepdims=True)
+    image = product(split_three(swap_order(start_ref[...], 4, 8)), gram, dot_nn)
+    basis_ref[...] = image * scale
+
+    def iterate(step, carry):
+        image = basis_ref[...]
+        parts = split_three(image)
+        cross = product(parts, parts, dot_nt)
+        ahead = product(parts, gram, dot_nn) * scale
+        inverse = inverse_cholesky(cross)
+        ahead = jnp.where(step < ITERS - 1, ahead, image)
+        basis_ref[...] = product(split_three(inverse), split_three(ahead), dot_nn)
         return carry
 
     lax.fori_loop(0, ITERS, iterate, 0)
+    for copy in copies:
+        copy.wait()
     basis = basis_ref[...]
-    factor_ref[...] = swap_order(basis, 8, 4)
-
     rank = basis.shape[0]
     both = jnp.concatenate(split(basis), axis=0)
-    for copy in copies:
-        copy.wait()
-    product = dot_nn(both, pieces[0]) + dot_nn(both, pieces[1])
-    product = product[:rank] + product[rank:]
+    core = dot_nn(both, pieces[0]) + dot_nn(both, pieces[1])
+    core = core[:rank] + core[rank:]
     flat = out_ref.reshape(rank * 16, LANES)
     for c in range(16):
-        flat[pl.ds(c, rank, stride=16), :] = product[:, c * LANES:(c + 1) * LANES]
+        flat[pl.ds(c, rank, stride=16), :] = core[:, c * LANES:(c + 1) * LANES]
+    factor_ref[...] = swap_order(basis, 8, 4)
 
 
 def finish(core, mine, other, start, pieces):
@@ -186,7 +218,7 @@
         ),
         scratch_shapes=[
             VMEM((2, 5, LANES, LANES), jnp.float32),
-            VMEM((512, 512), jnp.float32),
+            VMEM((3, 512, 512), jnp.bfloat16),
             VMEM(start.shape, jnp.float32),
             VMEM((2, 512, 2048), jnp.bfloat16),
             pltpu.SemaphoreType.DMA((2,)),
@@ -194,6 +226,31 @@
         compiler_params=pltpu.CompilerParams(vmem_limit_bytes=KERNEL_VMEM),
         name="finish",
     )(core, on_chip(mine), on_chip(other), on_chip(start), pltpu.with_memory_space_constraint(pieces, pltpu.HBM))
+
+
+def arrange_kernel(x_ref, out_ref, sems):
+    rows, outer = x_ref.shape[0], x_ref.shape[1]
+    copies = [
+        pltpu.make_async_copy(x_ref.at[r, x], out_ref.at[:, x, :, r], sems.at[r * outer + x])
+        for r in range(rows) for x in range(outer)
+    ]
+    for copy in copies:
+        copy.start()
+    for copy in copies:
+        copy.wait()
+
+
+def arrange(view):
+    rows, x, z, n = view.shape[:4]
+    return pl.pallas_call(
+        arrange_kernel,
+        in_specs=[pl.BlockSpec(memory_space=pltpu.HBM)],
+        out_specs=WHOLE,
+        out_shape=VMEM((z, x, n, rows, 8, LANES), jnp.float32),
+        scratch_shapes=[pltpu.SemaphoreType.DMA((rows * x,))],
+        compiler_params=pltpu.CompilerParams(vmem_limit_bytes=KERNEL_VMEM),
+        name="arrange",
+    )(pltpu.with_memory_space_constraint(view, pltpu.HBM))
 
 
 def exchange(x, axes):
@@ -218,8 +275,8 @@
     rows, cols = field.shape[0], field.shape[1]
     view = field.reshape(rows, cols, 2, LANES, 4)
     view = with_layout_constraint(view, Layout(major_to_minor=(0, 1, 2, 4, 3)))
-    view = view.transpose(1, 0, 2, 4, 3).reshape(4, 8, cols // 32, rows, 8, LANES)
-    view = view.transpose(1, 0, 2, 3, 4, 5).reshape(cols, rows, 8, LANES)
+    view = view.transpose(0, 1, 2, 4, 3).reshape(rows, 4, 8, cols // 32, 8, LANES)
+    view = arrange(view).reshape(cols, rows, 8, LANES)
     moved = exchange(view, ("z", "x", "c"))
     blocks = moved.reshape(64, cols // 64, rows * 8, LANES)
     packed, pieces = local_gram(blocks)

time: 173 us -> 169 us (0.977)
  local copies, waits for them, and re-layouts: 2.8 us -> 0.04 us
    pallas_call x1, Pallas kernels: 12.2 us -> 8.8 us  [finish(): pl.pallas_call(finish_kernel, in_specs=[pl.BlockSpec(memory_space=pltpu.S...]
    transpose x1 -> x0, local copies, waits for them, and re-layouts: 2.76 us -> none  [on_device(): view = view.transpose(1, 0, 2, 3, 4, 5).reshape(cols, rows, 8, LANES)]
    pallas_call x0 -> x1, Pallas kernels: none -> 2.54 us  [arrange(): pl.pallas_call(arrange_kernel, in_specs=[pl.BlockSpec(memory_space=pltpu....]
where the time goes in v4:
time: 169 us
  blocking collectives  144 us (85%)
  Pallas kernels  14.9 us (9%)
  starting transfers between devices  6.07 us (4%)
  waiting for transfers between devices  2.98 us (2%)
    all_to_all x4, blocking collectives, exchange(): return lax.all_to_all(x, axes, split_axis=0, concat_axis=0, tiled=True)  144 us
    pallas_call x1, Pallas kernels, finish(): pl.pallas_call(finish_kernel, in_specs=[pl.BlockSpec(memory_space=pltpu.S...  8.8 us
    ppermute x1, starting transfers between devices, sum_over_devices(): return (core.reshape(1), mine, lax.ppermute(mine, 'c', [(0, 1), (1, 0)]))  3.9 us
    pallas_call x1, Pallas kernels, local_gram(): pl.pallas_call(gram_kernel, in_specs=[WHOLE], out_specs=(WHOLE, pl.BlockS...  3.61 us
  transfers between devices with their start and end apart: 2, of which 2 were waited for; matrix products, arithmetic and copies ran while one was open for 0% of the time, Pallas kernels for 0%

profile of v4, /device:TPU:1, one launch (start us, length us, event | category | flops | bytes accessed | tf_op | source)
XLA Modules:
  0.0 168.9 jit_solution(10051032043091985159)
XLA Ops:
  0.6 2.5 %arrange.1 = f32[8,4,4,8,8,128]{5,4,3,2,1,0:T(8,128)S(1)} custom-call(f32[8,4,8,4,8,128]{5,4,3,2,1,0:T(8,128)} %bitcast.25), custom_call_target="tpu_custom_call" | custom-call | tf_op jit(solution)/shard_map/arrange/pallas_call | solution.py:245
  3.2 107.4 %all_to_all.20 = f32[128,8,8,128]{3,2,1,0:T(8,128)S(1)} all-to-all(f32[128,8,8,128]{3,2,1,0:T(8,128)S(1)} %bitcast.19), channel_id=1, replica_groups=mesh['y'=4,'x'=4,'z'=8,'c'=2] {'z','x','c'}, dimensions={0} | all-to-all | bytes 8388608 | tf_op jit(solution)/shard_map/all_to_all | solution.py:257
  110.6 0.0 copy-start
  110.6 3.6 %local_gram.1 = (f32[10,128,128]{2,1,0:T(8,128)S(1)}, bf16[2,512,2048]{2,1,0:T(8,128)(2,1)}) custom-call(f32[64,2,64,128]{3,2,1,0:T(8,128)S(1)} %bitcast.18), custom_call_target="tpu_custom_call" | custom-call | tf_op jit(solution)/shard_map/local_gram/pallas_call | solution.py:86
  114.2 2.2 %collective-permute-start = (f32[2,640,128]{2,1,0:T(8,128)S(1)}, f32[2,640,128]{2,1,0:T(8,128)S(1)}, u32[]{:S(2)}, u32[]{:S(2)}) collective-permute-start(f32[2,640,128]{2,1,0:T(8,128)S(1)} %bitcast.22), channel_id=1, source_target_pairs={{0,1},{1,0},{2,3},{3,2},{4,5},{5,4},{6,7},{7,6},{8,9},{9,8},{10,11... | collective-permute-start | bytes 1966088 | tf_op jit(solution)/shard_map/ppermute | solution.py:263
  116.4 1.7 %collective-permute-done = f32[2,640,128]{2,1,0:T(8,128)S(1)} collective-permute-done((f32[2,640,128]{2,1,0:T(8,128)S(1)}, f32[2,640,128]{2,1,0:T(8,128)S(1)}, u32[]{:S(2)}, u32[]{:S(2)}) %collective-permute-start) | collective-permute-done | bytes 655392 | tf_op jit(solution)/shard_map/ppermute | solution.py:263
  118.1 15.4 %all_to_all.21 = f32[16,40,128]{2,1,0:T(8,128)S(1)} all-to-all(f32[16,40,128]{2,1,0:T(8,128)S(1)} %bitcast.26), channel_id=1, replica_groups=mesh['y'=4,'x'=4,'z'=8,'c'=2] {'y','x'}, dimensions={0} | all-to-all | bytes 655360 | tf_op jit(solution)/shard_map/all_to_all | solution.py:257
  133.5 10.8 %all_to_all.22 = f32[8,40,128]{2,1,0:T(8,128)S(1)} all-to-all(f32[8,40,128]{2,1,0:T(8,128)S(1)} %broadcast_in_dim.4), channel_id=1, replica_groups=mesh['y'=4,'x'=4,'z'=8,'c'=2] {'z'}, dimensions={0} | all-to-all | bytes 327680 | tf_op jit(solution)/shard_map/all_to_all | solution.py:257
  144.4 10.6 %all_to_all.23 = f32[16,40,128]{2,1,0:T(8,128)S(1)} all-to-all(f32[16,40,128]{2,1,0:T(8,128)S(1)} %broadcast_in_dim.5), channel_id=1, replica_groups=mesh['y'=4,'x'=4,'z'=8,'c'=2] {'y','x'}, dimensions={0} | all-to-all | bytes 655360 | tf_op jit(solution)/shard_map/all_to_all | solution.py:257
  154.9 3.9 %collective-permute-start.1 = (f32[5,128,128]{2,1,0:T(8,128)S(1)}, f32[5,128,128]{2,1,0:T(8,128)S(1)}, u32[]{:S(2)}, u32[]{:S(2)}) collective-permute-start(f32[5,128,128]{2,1,0:T(8,128)S(1)} %bitcast.20), channel_id=1, source_target_pairs={{0,1},{1,0},{2,3},{3,2},{4,5},{5,4},{6,7},{7,6},{8,9},{9,8},{10,11... | collective-permute-start | bytes 983048 | tf_op jit(solution)/shard_map/ppermute | solution.py:271
  158.8 1.3 collective-permute-done.1.other_ref
  160.1 0.0 copy-done
  160.1 8.8 %finish.1 = (f32[64,512]{1,0:T(8,128)}, f32[64,2,8,128]{3,2,1,0:T(8,128)}) custom-call(s32[1]{0:T(128)} %bitcast.core_ref, f32[5,128,128]{2,1,0:T(8,128)S(1)} %bitcast.21, f32[5,128,128]{2,1,0:T(8,128)S(1)} %collective-permute-done.1.other_ref, f32[64,512]{1,0:T(8,128)S(1)} %bitcast.24, bf16[2,512,2048]{2,1,0:T(8,128)(2,1)} %get-tuple-element.7.pieces_ref), custom_call_target="tpu_custom_call" | custom-call | tf_op jit(solution)/shard_map/finish/pallas_call | solution.py:208
  (5 shorter events, 0.1 us)
Async XLA Ops:
  110.6 49.5 %copy-start = (f32[512,64]{0,1:T(8,128)S(1)}, f32[512,64]{0,1:T(8,128)}, u32[]{:S(2)}) copy-start(f32[512,64]{0,1:T(8,128)} %param.3) | copy-start | bytes 393220
  114.2 3.9 %collective-permute-start = (f32[2,640,128]{2,1,0:T(8,128)S(1)}, f32[2,640,128]{2,1,0:T(8,128)S(1)}, u32[]{:S(2)}, u32[]{:S(2)}) collective-permute-start(f32[2,640,128]{2,1,0:T(8,128)S(1)} %bitcast.22), channel_id=1, source_target_pairs={{0,1},{1,0},{2,3},{3,2},{4,5},{5,4},{6,7},{7,6},{8,9},{9,8},{10,11... | collective-permute-start | bytes 1966088 | tf_op jit(solution)/shard_map/ppermute | solution.py:263
  154.9 5.2 %collective-permute-start.1 = (f32[5,128,128]{2,1,0:T(8,128)S(1)}, f32[5,128,128]{2,1,0:T(8,128)S(1)}, u32[]{:S(2)}, u32[]{:S(2)}) collective-permute-start(f32[5,128,128]{2,1,0:T(8,128)S(1)} %bitcast.20), channel_id=1, source_target_pairs={{0,1},{1,0},{2,3},{3,2},{4,5},{5,4},{6,7},{7,6},{8,9},{9,8},{10,11... | collective-permute-start | bytes 983048 | tf_op jit(solution)/shard_map/ppermute | solution.py:271

commit v5 on v4

--- a/solution.py
+++ b/solution.py
@@ -12,6 +12,7 @@
 PACK = tuple((i, j) for i in range(4) for j in range(i, 4))
 VMEM = pltpu.VMEM
 WHOLE = pl.BlockSpec(memory_space=VMEM)
+HBM = pl.BlockSpec(memory_space=pltpu.HBM)
 HIGHEST = lax.Precision.HIGHEST
 
 
@@ -69,11 +70,16 @@
     ]
     for copy in copies:
         copy.start()
-    mixed = dot_nt(jnp.concatenate([high, mid], axis=1), jnp.concatenate([mid, mid * 0.5], axis=1))
+    mixed = dot_nt(
+        jnp.concatenate([high, mid], axis=1), jnp.concatenate([mid, mid * 0.5], axis=1)
+    )
     square = dot_nt(high, high)
+
+    core = lax.axis_index("c")
+    places = (core, 1 - core)
     for n, (i, j) in enumerate(PACK):
         row, col = slice(i * LANES, (i + 1) * LANES), slice(j * LANES, (j + 1) * LANES)
-        packed_ref[n] = square[row, col] + mixed[row, col] + mixed[col, row].T
+        packed_ref[places[n // 5], n % 5] = square[row, col] + mixed[row, col] + mixed[col, row].T
     for copy in copies:
         copy.wait()
 
@@ -83,14 +89,12 @@
 
 
 def local_gram(blocks):
+    halves = VMEM((2, len(PACK) // 2, LANES, LANES), jnp.float32)
     return pl.pallas_call(
         gram_kernel,
         in_specs=[WHOLE],
-        out_specs=(WHOLE, pl.BlockSpec(memory_space=pltpu.HBM)),
-        out_shape=(
-            VMEM((len(PACK), LANES, LANES), jnp.float32),
-            pltpu.HBM((2, 512, 2048), jnp.bfloat16),
-        ),
+        out_specs=(WHOLE, HBM),
+        out_shape=(halves, pltpu.HBM((2, 512, 2048), jnp.bfloat16)),
         scratch_shapes=[VMEM((2, 512, 2048), jnp.bfloat16), pltpu.SemaphoreType.DMA((2,))],
         compiler_params=pltpu.CompilerParams(vmem_limit_bytes=KERNEL_VMEM),
         name="local_gram",
@@ -152,15 +156,15 @@
 
 
 def finish_kernel(
-    core_ref, mine_ref, other_ref, start_ref, pieces_ref, factor_ref, out_ref,
-    packed, gram, basis_ref, pieces, sems,
+    mine_ref, other_ref, start_ref, pieces_ref, factor_ref, out_ref,
+    packed, gram, basis_ref, pieces, sems, factor, slab, out_sems,
 ):
     copies = [
         pltpu.make_async_copy(pieces_ref.at[n], pieces.at[n], sems.at[n]) for n in range(2)
     ]
     for copy in copies:
         copy.start()
-    core = core_ref[0]
+    core = lax.axis_index("c")
     packed[core] = mine_ref[...]
     packed[1 - core] = other_ref[...]
     for n, (i, j) in enumerate(PACK):
@@ -179,42 +183,50 @@
     image = product(split_three(swap_order(start_ref[...], 4, 8)), gram, dot_nn)
     basis_ref[...] = image * scale
 
-    def iterate(step, carry):
-        image = basis_ref[...]
-        parts = split_three(image)
+    def iterate(_, carry):
+        parts = split_three(basis_ref[...])
         cross = product(parts, parts, dot_nt)
         ahead = product(parts, gram, dot_nn) * scale
         inverse = inverse_cholesky(cross)
-        ahead = jnp.where(step < ITERS - 1, ahead, image)
         basis_ref[...] = product(split_three(inverse), split_three(ahead), dot_nn)
         return carry
 
-    lax.fori_loop(0, ITERS, iterate, 0)
+    lax.fori_loop(0, ITERS - 1, iterate, 0)
+    parts = split_three(basis_ref[...])
+    inverse = inverse_cholesky(product(parts, parts, dot_nt))
+    basis = product(split_three(inverse), parts, dot_nn)
     for copy in copies:
         copy.wait()
-    basis = basis_ref[...]
     rank = basis.shape[0]
+    factor[...] = swap_order(basis, 8, 4)
+    outgoing = [pltpu.make_async_copy(factor, factor_ref, out_sems.at[2])]
+    outgoing[0].start()
     both = jnp.concatenate(split(basis), axis=0)
-    core = dot_nn(both, pieces[0]) + dot_nn(both, pieces[1])
-    core = core[:rank] + core[rank:]
-    flat = out_ref.reshape(rank * 16, LANES)
-    for c in range(16):
-        flat[pl.ds(c, rank, stride=16), :] = core[:, c * LANES:(c + 1) * LANES]
-    factor_ref[...] = swap_order(basis, 8, 4)
-
-
-def finish(core, mine, other, start, pieces):
+    for part in range(2):
+        cols = slice(part * 1024, (part + 1) * 1024)
+        core = dot_nn(both, pieces[0, :, cols]) + dot_nn(both, pieces[1, :, cols])
+        core = core[:rank] + core[rank:]
+        flat = slab.at[part].reshape(rank * 8, LANES)
+        for c in range(8):
+            flat[pl.ds(c, rank, stride=8), :] = core[:, c * LANES:(c + 1) * LANES]
+        outgoing.append(pltpu.make_async_copy(slab.at[part], out_ref.at[:, part], out_sems.at[part]))
+        outgoing[-1].start()
+    for copy in outgoing:
+        copy.wait()
+
+
+def finish(mine, other, start, pieces):
     rank = start.shape[0]
     return pl.pallas_call(
         finish_kernel,
         in_specs=[
-            pl.BlockSpec(memory_space=pltpu.SMEM), WHOLE, WHOLE, WHOLE,
+            WHOLE, WHOLE, WHOLE,
             pl.BlockSpec(memory_space=pltpu.HBM),
         ],
-        out_specs=(WHOLE, WHOLE),
+        out_specs=(HBM, HBM),
         out_shape=(
-            jax.ShapeDtypeStruct(start.shape, jnp.float32),
-            jax.ShapeDtypeStruct((rank, 2, 8, LANES), jnp.float32),
+            pltpu.HBM(start.shape, jnp.float32),
+            pltpu.HBM((rank, 2, 8, LANES), jnp.float32),
         ),
         scratch_shapes=[
             VMEM((2, 5, LANES, LANES), jnp.float32),
@@ -222,10 +234,13 @@
             VMEM(start.shape, jnp.float32),
             VMEM((2, 512, 2048), jnp.bfloat16),
             pltpu.SemaphoreType.DMA((2,)),
+            VMEM(start.shape, jnp.float32),
+            VMEM((2, rank, 8, LANES), jnp.float32),
+            pltpu.SemaphoreType.DMA((3,)),
         ],
         compiler_params=pltpu.CompilerParams(vmem_limit_bytes=KERNEL_VMEM),
         name="finish",
-    )(core, on_chip(mine), on_chip(other), on_chip(start), pltpu.with_memory_space_constraint(pieces, pltpu.HBM))
+    )(on_chip(mine), on_chip(other), on_chip(start), pltpu.with_memory_space_constraint(pieces, pltpu.HBM))
 
 
 def arrange_kernel(x_ref, out_ref, sems):
@@ -257,18 +272,16 @@
     return lax.all_to_all(x, axes, split_axis=0, concat_axis=0, tiled=True)
 
 
-def sum_over_devices(packed):
-    core = lax.axis_index("c")
-    flat = packed.reshape(2, 640, LANES)
-    theirs = lax.ppermute(flat, "c", [(0, 1), (1, 0)])
-    half = lax.dynamic_index_in_dim(flat, core, 0, False) + lax.dynamic_index_in_dim(theirs, core, 0, False)
+def sum_over_devices(mine, theirs):
+    swap = [(0, 1), (1, 0)]
+    half = mine + lax.ppermute(theirs, "c", swap)
     parts = exchange(half.reshape(16, 40, LANES), ("y", "x"))
     part = jnp.sum(parts, axis=0)
     parts = exchange(jnp.broadcast_to(part[None], (8, 40, LANES)), "z")
     part = jnp.sum(parts, axis=0)
     half = exchange(jnp.broadcast_to(part[None], (16, 40, LANES)), ("y", "x"))
     mine = half.reshape(5, LANES, LANES)
-    return core.reshape(1), mine, lax.ppermute(mine, "c", [(0, 1), (1, 0)])
+    return mine, lax.ppermute(mine, "c", swap)
 
 
 def on_device(field, start_basis):
@@ -279,9 +292,9 @@
     view = arrange(view).reshape(cols, rows, 8, LANES)
     moved = exchange(view, ("z", "x", "c"))
     blocks = moved.reshape(64, cols // 64, rows * 8, LANES)
-    packed, pieces = local_gram(blocks)
-    core, mine, other = sum_over_devices(packed)
-    factor, out = finish(core, mine, other, start_basis.T, pieces)
+    halves, pieces = local_gram(blocks)
+    mine, other = sum_over_devices(halves[0], halves[1])
+    factor, out = finish(mine, other, start_basis.T, pieces)
     rank = factor.shape[0]
     out = out.reshape(rank, cols // 64, 2, 4, LANES).transpose(0, 1, 2, 4, 3)
     return factor.T, out.reshape(rank, cols // 64, 256, 4)

time: 169 us -> 169 us (level)
  no operation moved by 1% of the time
where the time goes in v5:
time: 169 us; the launch traced here: 168 us
  blocking collectives  144 us (85%)
  Pallas kernels  14.9 us (9%)
  starting transfers between devices  6.07 us (4%)
  waiting for transfers between devices  2.51 us (1%)
    all_to_all x4, blocking collectives, exchange(): return lax.all_to_all(x, axes, split_axis=0, concat_axis=0, tiled=True)  144 us
    pallas_call x1, Pallas kernels, finish(): pl.pallas_call(finish_kernel, in_specs=[WHOLE, WHOLE, WHOLE, pl.BlockSpec...  8.72 us
    ppermute x1, starting transfers between devices, sum_over_devices(): return (mine, lax.ppermute(mine, 'c', swap))  3.9 us
    pallas_call x1, Pallas kernels, local_gram(): pl.pallas_call(gram_kernel, in_specs=[WHOLE], out_specs=(WHOLE, HBM), out...  3.61 us
  transfers between devices with their start and end apart: 2, of which 2 were waited for; matrix products, arithmetic and copies ran while one was open for 0% of the time, Pallas kernels for 0%

profile of v5, /device:TPU:1, one launch (start us, length us, event | category | flops | bytes accessed | tf_op | source)
XLA Modules:
  0.0 168.4 jit_solution(13678038477860414349)
XLA Ops:
  0.6 2.5 %arrange.1 = f32[8,4,4,8,8,128]{5,4,3,2,1,0:T(8,128)S(1)} custom-call(f32[8,4,8,4,8,128]{5,4,3,2,1,0:T(8,128)} %bitcast.25), custom_call_target="tpu_custom_call" | custom-call | tf_op jit(solution)/shard_map/arrange/pallas_call | solution.py:260
  3.2 107.4 %all_to_all.20 = f32[128,8,8,128]{3,2,1,0:T(8,128)S(1)} all-to-all(f32[128,8,8,128]{3,2,1,0:T(8,128)S(1)} %bitcast.21), channel_id=1, replica_groups=mesh['y'=4,'x'=4,'z'=8,'c'=2] {'z','x','c'}, dimensions={0} | all-to-all | bytes 8388608 | tf_op jit(solution)/shard_map/all_to_all | solution.py:272
  110.6 0.0 copy-start
  110.6 3.6 %local_gram.1 = (f32[2,5,128,128]{3,2,1,0:T(8,128)S(1)}, bf16[2,512,2048]{2,1,0:T(8,128)(2,1)}) custom-call(f32[64,2,64,128]{3,2,1,0:T(8,128)S(1)} %bitcast.20), custom_call_target="tpu_custom_call" | custom-call | tf_op jit(solution)/shard_map/local_gram/pallas_call | solution.py:93
  114.2 2.2 %collective-permute-start = (f32[5,128,128]{2,1,0:T(8,128)S(1)}, f32[5,128,128]{2,1,0:T(8,128)S(1)}, u32[]{:S(2)}, u32[]{:S(2)}) collective-permute-start(f32[5,128,128]{2,1,0:T(8,128)S(1)} %slice_bitcast_fusion), channel_id=1, source_target_pairs={{0,1},{1,0},{2,3},{3,2},{4,5},{5,4},{6,7},{7,6},{8,9},{9,8},{10,11... | collective-permute-start | bytes 983048 | tf_op jit(solution)/shard_map/ppermute | solution.py:277
  116.4 1.3 collective-permute-done
  117.7 15.4 %all_to_all.21 = f32[16,40,128]{2,1,0:T(8,128)S(1)} all-to-all(f32[16,40,128]{2,1,0:T(8,128)S(1)} %bitcast.26), channel_id=1, replica_groups=mesh['y'=4,'x'=4,'z'=8,'c'=2] {'y','x'}, dimensions={0} | all-to-all | bytes 655360 | tf_op jit(solution)/shard_map/all_to_all | solution.py:272
  133.1 10.8 %all_to_all.22 = f32[8,40,128]{2,1,0:T(8,128)S(1)} all-to-all(f32[8,40,128]{2,1,0:T(8,128)S(1)} %broadcast_in_dim.4), channel_id=1, replica_groups=mesh['y'=4,'x'=4,'z'=8,'c'=2] {'z'}, dimensions={0} | all-to-all | bytes 327680 | tf_op jit(solution)/shard_map/all_to_all | solution.py:272
  143.9 10.6 %all_to_all.23 = f32[16,40,128]{2,1,0:T(8,128)S(1)} all-to-all(f32[16,40,128]{2,1,0:T(8,128)S(1)} %broadcast_in_dim.5), channel_id=1, replica_groups=mesh['y'=4,'x'=4,'z'=8,'c'=2] {'y','x'}, dimensions={0} | all-to-all | bytes 655360 | tf_op jit(solution)/shard_map/all_to_all | solution.py:272
  154.5 3.9 %collective-permute-start.1 = (f32[5,128,128]{2,1,0:T(8,128)S(1)}, f32[5,128,128]{2,1,0:T(8,128)S(1)}, u32[]{:S(2)}, u32[]{:S(2)}) collective-permute-start(f32[5,128,128]{2,1,0:T(8,128)S(1)} %bitcast.22), channel_id=1, source_target_pairs={{0,1},{1,0},{2,3},{3,2},{4,5},{5,4},{6,7},{7,6},{8,9},{9,8},{10,11... | collective-permute-start | bytes 983048 | tf_op jit(solution)/shard_map/ppermute | solution.py:284
  158.4 1.3 collective-permute-done.1.other_ref
  159.7 0.0 copy-done
  159.7 8.7 %finish.1 = (f32[64,512]{1,0:T(8,128)}, f32[64,2,8,128]{3,2,1,0:T(8,128)}) custom-call(f32[5,128,128]{2,1,0:T(8,128)S(1)} %bitcast.23, f32[5,128,128]{2,1,0:T(8,128)S(1)} %collective-permute-done.1.other_ref, f32[64,512]{1,0:T(8,128)S(1)} %bitcast.24, bf16[2,512,2048]{2,1,0:T(8,128)(2,1)} %get-tuple-element.7.pieces_ref), custom_call_target="tpu_custom_call" | custom-call | tf_op jit(solution)/shard_map/finish/pallas_call | solution.py:220
  (6 shorter events, 0.1 us)
Async XLA Ops:
  110.6 49.1 %copy-start = (f32[512,64]{0,1:T(8,128)S(1)}, f32[512,64]{0,1:T(8,128)}, u32[]{:S(2)}) copy-start(f32[512,64]{0,1:T(8,128)} %param.3) | copy-start | bytes 393220
  114.2 3.4 %collective-permute-start = (f32[5,128,128]{2,1,0:T(8,128)S(1)}, f32[5,128,128]{2,1,0:T(8,128)S(1)}, u32[]{:S(2)}, u32[]{:S(2)}) collective-permute-start(f32[5,128,128]{2,1,0:T(8,128)S(1)} %slice_bitcast_fusion), channel_id=1, source_target_pairs={{0,1},{1,0},{2,3},{3,2},{4,5},{5,4},{6,7},{7,6},{8,9},{9,8},{10,11... | collective-permute-start | bytes 983048 | tf_op jit(solution)/shard_map/ppermute | solution.py:277
  154.5 5.2 %collective-permute-start.1 = (f32[5,128,128]{2,1,0:T(8,128)S(1)}, f32[5,128,128]{2,1,0:T(8,128)S(1)}, u32[]{:S(2)}, u32[]{:S(2)}) collective-permute-start(f32[5,128,128]{2,1,0:T(8,128)S(1)} %bitcast.22), channel_id=1, source_target_pairs={{0,1},{1,0},{2,3},{3,2},{4,5},{5,4},{6,7},{7,6},{8,9},{9,8},{10,11... | collective-permute-start | bytes 983048 | tf_op jit(solution)/shard_map/ppermute | solution.py:284

commit v6 on v5

--- a/solution.py
+++ b/solution.py
@@ -61,20 +61,23 @@
     return one[:n] + (one[n:2 * n] + two[:n]) + (one[2 * n:] + two[n:] + three)
 
 
-def gram_kernel(x_ref, packed_ref, pieces_ref, pieces, sems):
+def gram_kernel(x_ref, packed_ref, pieces_ref, left, right, sems):
     high, mid = split(gather_columns(x_ref))
-    pieces[0] = high
-    pieces[1] = mid
+    columns = high.shape[1]
+    left[:, :columns] = high
+    left[:, columns:] = mid
+    right[:, :columns] = mid
+    right[:, columns:] = mid * 0.5
     copies = [
-        pltpu.make_async_copy(pieces.at[n], pieces_ref.at[n], sems.at[n]) for n in range(2)
+        pltpu.make_async_copy(
+            left.at[:, n * columns:(n + 1) * columns], pieces_ref.at[n], sems.at[n]
+        )
+        for n in range(2)
     ]
     for copy in copies:
         copy.start()
-    mixed = dot_nt(
-        jnp.concatenate([high, mid], axis=1), jnp.concatenate([mid, mid * 0.5], axis=1)
-    )
-    square = dot_nt(high, high)
-
+    mixed = dot_nt(left[...], right[...])
+    square = dot_nt(left[:, :columns], left[:, :columns])
     core = lax.axis_index("c")
     places = (core, 1 - core)
     for n, (i, j) in enumerate(PACK):
@@ -95,7 +98,11 @@
         in_specs=[WHOLE],
         out_specs=(WHOLE, HBM),
         out_shape=(halves, pltpu.HBM((2, 512, 2048), jnp.bfloat16)),
-        scratch_shapes=[VMEM((2, 512, 2048), jnp.bfloat16), pltpu.SemaphoreType.DMA((2,))],
+        scratch_shapes=[
+            VMEM((512, 4096), jnp.bfloat16),
+            VMEM((512, 4096), jnp.bfloat16),
+            pltpu.SemaphoreType.DMA((2,)),
+        ],
         compiler_params=pltpu.CompilerParams(vmem_limit_bytes=KERNEL_VMEM),
         name="local_gram",
     )(on_chip(blocks))
@@ -275,11 +282,11 @@
 def sum_over_devices(mine, theirs):
     swap = [(0, 1), (1, 0)]
     half = mine + lax.ppermute(theirs, "c", swap)
-    parts = exchange(half.reshape(16, 40, LANES), ("y", "x"))
+    parts = exchange(half.reshape(16, 40, LANES), ("x", "y"))
     part = jnp.sum(parts, axis=0)
     parts = exchange(jnp.broadcast_to(part[None], (8, 40, LANES)), "z")
     part = jnp.sum(parts, axis=0)
-    half = exchange(jnp.broadcast_to(part[None], (16, 40, LANES)), ("y", "x"))
+    half = exchange(jnp.broadcast_to(part[None], (16, 40, LANES)), ("x", "y"))
     mine = half.reshape(5, LANES, LANES)
     return mine, lax.ppermute(mine, "c", swap)
 

time: 169 us -> 169 us (level)
  no operation moved by 1% of the time
where the time goes in v6:
time: 169 us
  blocking collectives  144 us (85%)
  Pallas kernels  14.8 us (9%)
  starting transfers between devices  6.15 us (4%)
  waiting for transfers between devices  2.51 us (1%)
    all_to_all x4, blocking collectives, exchange(): return lax.all_to_all(x, axes, split_axis=0, concat_axis=0, tiled=True)  144 us
    pallas_call x1, Pallas kernels, finish(): pl.pallas_call(finish_kernel, in_specs=[WHOLE, WHOLE, WHOLE, pl.BlockSpec...  8.73 us
    ppermute x1, starting transfers between devices, sum_over_devices(): return (mine, lax.ppermute(mine, 'c', swap))  3.98 us
    pallas_call x1, Pallas kernels, local_gram(): pl.pallas_call(gram_kernel, in_specs=[WHOLE], out_specs=(WHOLE, HBM), out...  3.56 us
  transfers between devices with their start and end apart: 2, of which 2 were waited for; matrix products, arithmetic and copies ran while one was open for 0% of the time, Pallas kernels for 0%

profile of v6, /device:TPU:1, one launch (start us, length us, event | category | flops | bytes accessed | tf_op | source)
XLA Modules:
  0.0 168.5 jit_solution(16369521647752993312)
XLA Ops:
  0.6 2.5 %arrange.1 = f32[8,4,4,8,8,128]{5,4,3,2,1,0:T(8,128)S(1)} custom-call(f32[8,4,8,4,8,128]{5,4,3,2,1,0:T(8,128)} %bitcast.25), custom_call_target="tpu_custom_call" | custom-call | tf_op jit(solution)/shard_map/arrange/pallas_call | solution.py:267
  3.2 107.4 %all_to_all.20 = f32[128,8,8,128]{3,2,1,0:T(8,128)S(1)} all-to-all(f32[128,8,8,128]{3,2,1,0:T(8,128)S(1)} %bitcast.21), channel_id=1, replica_groups=mesh['y'=4,'x'=4,'z'=8,'c'=2] {'z','x','c'}, dimensions={0} | all-to-all | bytes 8388608 | tf_op jit(solution)/shard_map/all_to_all | solution.py:279
  110.6 0.0 copy-start
  110.6 3.6 %local_gram.1 = (f32[2,5,128,128]{3,2,1,0:T(8,128)S(1)}, bf16[2,512,2048]{2,1,0:T(8,128)(2,1)}) custom-call(f32[64,2,64,128]{3,2,1,0:T(8,128)S(1)} %bitcast.20), custom_call_target="tpu_custom_call" | custom-call | tf_op jit(solution)/shard_map/local_gram/pallas_call | solution.py:96
  114.2 2.2 %collective-permute-start = (f32[5,128,128]{2,1,0:T(8,128)S(1)}, f32[5,128,128]{2,1,0:T(8,128)S(1)}, u32[]{:S(2)}, u32[]{:S(2)}) collective-permute-start(f32[5,128,128]{2,1,0:T(8,128)S(1)} %slice_bitcast_fusion), channel_id=1, source_target_pairs={{0,1},{1,0},{2,3},{3,2},{4,5},{5,4},{6,7},{7,6},{8,9},{9,8},{10,11... | collective-permute-start | bytes 983048 | tf_op jit(solution)/shard_map/ppermute | solution.py:284
  116.4 1.3 collective-permute-done
  117.7 14.5 %all_to_all.21 = f32[16,40,128]{2,1,0:T(8,128)S(1)} all-to-all(f32[16,40,128]{2,1,0:T(8,128)S(1)} %bitcast.26), channel_id=1, replica_groups=mesh['y'=4,'x'=4,'z'=8,'c'=2] {'x','y'}, dimensions={0} | all-to-all | bytes 655360 | tf_op jit(solution)/shard_map/all_to_all | solution.py:279
  132.2 10.8 %all_to_all.22 = f32[8,40,128]{2,1,0:T(8,128)S(1)} all-to-all(f32[8,40,128]{2,1,0:T(8,128)S(1)} %broadcast_in_dim.4), channel_id=1, replica_groups=mesh['y'=4,'x'=4,'z'=8,'c'=2] {'z'}, dimensions={0} | all-to-all | bytes 327680 | tf_op jit(solution)/shard_map/all_to_all | solution.py:279
  143.0 11.5 %all_to_all.23 = f32[16,40,128]{2,1,0:T(8,128)S(1)} all-to-all(f32[16,40,128]{2,1,0:T(8,128)S(1)} %broadcast_in_dim.5), channel_id=1, replica_groups=mesh['y'=4,'x'=4,'z'=8,'c'=2] {'x','y'}, dimensions={0} | all-to-all | bytes 655360 | tf_op jit(solution)/shard_map/all_to_all | solution.py:279
  154.5 4.0 %collective-permute-start.1 = (f32[5,128,128]{2,1,0:T(8,128)S(1)}, f32[5,128,128]{2,1,0:T(8,128)S(1)}, u32[]{:S(2)}, u32[]{:S(2)}) collective-permute-start(f32[5,128,128]{2,1,0:T(8,128)S(1)} %bitcast.22), channel_id=1, source_target_pairs={{0,1},{1,0},{2,3},{3,2},{4,5},{5,4},{6,7},{7,6},{8,9},{9,8},{10,11... | collective-permute-start | bytes 983048 | tf_op jit(solution)/shard_map/ppermute | solution.py:291
  158.5 1.3 collective-permute-done.1.other_ref
  159.8 0.0 copy-done
  159.8 8.7 %finish.1 = (f32[64,512]{1,0:T(8,128)}, f32[64,2,8,128]{3,2,1,0:T(8,128)}) custom-call(f32[5,128,128]{2,1,0:T(8,128)S(1)} %bitcast.23, f32[5,128,128]{2,1,0:T(8,128)S(1)} %collective-permute-done.1.other_ref, f32[64,512]{1,0:T(8,128)S(1)} %bitcast.24, bf16[2,512,2048]{2,1,0:T(8,128)(2,1)} %get-tuple-element.7.pieces_ref), custom_call_target="tpu_custom_call" | custom-call | tf_op jit(solution)/shard_map/finish/pallas_call | solution.py:227
  (6 shorter events, 0.1 us)
Async XLA Ops:
  110.6 49.2 %copy-start = (f32[512,64]{0,1:T(8,128)S(1)}, f32[512,64]{0,1:T(8,128)}, u32[]{:S(2)}) copy-start(f32[512,64]{0,1:T(8,128)} %param.3) | copy-start | bytes 393220
  114.2 3.4 %collective-permute-start = (f32[5,128,128]{2,1,0:T(8,128)S(1)}, f32[5,128,128]{2,1,0:T(8,128)S(1)}, u32[]{:S(2)}, u32[]{:S(2)}) collective-permute-start(f32[5,128,128]{2,1,0:T(8,128)S(1)} %slice_bitcast_fusion), channel_id=1, source_target_pairs={{0,1},{1,0},{2,3},{3,2},{4,5},{5,4},{6,7},{7,6},{8,9},{9,8},{10,11... | collective-permute-start | bytes 983048 | tf_op jit(solution)/shard_map/ppermute | solution.py:284
  154.5 5.2 %collective-permute-start.1 = (f32[5,128,128]{2,1,0:T(8,128)S(1)}, f32[5,128,128]{2,1,0:T(8,128)S(1)}, u32[]{:S(2)}, u32[]{:S(2)}) collective-permute-start(f32[5,128,128]{2,1,0:T(8,128)S(1)} %bitcast.22), channel_id=1, source_target_pairs={{0,1},{1,0},{2,3},{3,2},{4,5},{5,4},{6,7},{7,6},{8,9},{9,8},{10,11... | collective-permute-start | bytes 983048 | tf_op jit(solution)/shard_map/ppermute | solution.py:291
